TPU v7x, 256 devices: a whole 4x4x8 slice. The times are simulated.
256 devices in a mesh: frame: 8 (over x, y_lo), pos: 32 (over z, y_hi, core).
Axes of the slice: x: 4, y: 4 (y_hi: 2, y_lo: 2; y = y_hi * 2 + y_lo), z: 8, core: 2. Of those that a mesh axis runs over, the one named last changes fastest.
Arguments:
- frames_in: bfloat16 [512, 256, 512], P('frame', 'pos'), may hold values from -40 to 40
- attn_gain: float32 [512], replicated, may hold values from 0.5 to 1.5
- w_query: bfloat16 [512, 512], replicated, may hold values from -4 to 4
- w_key: bfloat16 [512, 512], replicated, may hold values from -4 to 4
- w_value: bfloat16 [512, 512], replicated, may hold values from -0.25 to 0.25
- w_output: bfloat16 [512, 512], replicated, may hold values from -0.25 to 0.25
- moe_gain: float32 [512], replicated, may hold values from 0.5 to 1.5
- dispatch_keys: bfloat16 [512, 1024], replicated, may hold values from -10 to 10
- w_in: bfloat16 [32, 512, 1024], P('pos'), may hold values from -0.25 to 0.25
- w_out: bfloat16 [32, 1024, 512], P('pos'), may hold values from -0.125 to 0.125
Outputs:
- frames_out: bfloat16 [512, 256, 512], P('frame', 'pos')
All inputs are finite; a program needn't handle non-finite values.
Results may differ from a plain program's by a relative error of at most 0.0052.
Values may be sent and summed in bfloat16 or wider, within the bound.
No kernel may reach another device: no remote copies, remote signals or barrier semaphores. Data moves between devices by JAX's collectives and lax.ppermute only.
A program may use at most 64 MiB of HBM per device.

v0:
```python
import jax
import jax.numpy as jnp
from jax import lax
from jax.sharding import PartitionSpec as P

HEADS = 8
EXPERTS = 16
SLOTS = 64


EPS = 1e-06
LOGIT_SCALE = 3.0
MASKED = -1e30


def copy_for_each(shard, axis):
    copies = jnp.broadcast_to(shard, (lax.axis_size(axis), *shard.shape))
    return lax.all_to_all(copies, axis, split_axis=0, concat_axis=0, tiled=True)


def collected_together(shard, axis):
    leaves = jax.tree.leaves(shard)
    sequence = sorted(range(len(leaves)), key=lambda k: -leaves[k].size)
    width = (1, *leaves[sequence[0]].shape)[-1]
    lines = [
        jnp.pad(leaves[k].reshape(-1), (0, -leaves[k].size % width)).reshape(-1, width)
        for k in sequence
    ]
    both, at, found = (copy_for_each(jnp.concatenate(lines), axis), 0, {})
    for k, line in zip(sequence, lines):
        piece = both[:, at : at + len(line)].reshape(len(both), -1)
        found[k] = piece[:, : leaves[k].size].reshape(-1, *leaves[k].shape)
        at += len(line)
    numbers = iter(range(len(leaves)))
    return jax.tree.map(lambda _: found[next(numbers)], shard)


def combined_pairwise(pieces, combine):
    while len(jax.tree.leaves(pieces)[0]) > 1:
        pieces = jax.vmap(combine)(
            *(jax.tree.map(lambda part: part[side::2], pieces) for side in (0, 1))
        )
    return jax.tree.map(lambda part: part[0], pieces)


def merged(shard, axis, combine):
    pieces = collected_together(shard, axis)
    return combined_pairwise(pieces, combine)


def in_blocks(shard, dim, length):
    before, after = (shard.shape[:dim], shard.shape[dim + 1 :])
    return jnp.moveaxis(shard.reshape(*before, length, -1, *after), dim, 0)


def sum_at_owner(shard, axis, dim):
    length = lax.axis_size(axis)
    blocks = lax.all_to_all(in_blocks(shard, dim, length), axis, 0, 0, tiled=True)
    return jnp.sum(blocks.astype(jnp.float32), axis=0)


def from_partner(block, axis, apart):
    count = lax.axis_size(axis)
    route = []
    for low in range(count):
        high = low | 1 << apart
        if high != low and high < count:
            route += [(low, high), (high, low)]
    return lax.ppermute(block, axis, route)


def in_order(blocks, dim):
    blocks = jnp.moveaxis(blocks, 0, dim)
    dims = blocks.shape
    return blocks.reshape(*dims[:dim], dims[dim] * dims[dim + 1], *dims[dim + 2 :])


def collect(shard, axis, dim):
    return in_order(copy_for_each(shard, axis), dim)


def rms_scale(values_in, gain):
    values_in = values_in.astype(jnp.float32)
    mean_sq = jnp.mean(values_in * values_in, axis=-1, keepdims=True)
    return values_in * lax.rsqrt(mean_sq + EPS) * gain


def project(rows_in, weights):
    return jnp.dot(rows_in, weights, preferred_element_type=jnp.float32).astype(jnp.bfloat16)


def softmax_rows(scores, axis_index):
    largest = jnp.max(scores, axis=axis_index, keepdims=True)
    weights = jnp.exp(scores - largest)
    return (weights / jnp.sum(weights, axis=axis_index, keepdims=True)).astype(jnp.bfloat16)


def attend(queries, keys_block, values_block):
    frame_count = queries.shape[0]
    score_scale = queries.shape[3] ** (-0.5)
    causal = jnp.arange(frame_count)[:, None] >= jnp.arange(frame_count)[None, :]

    def one_head(triple):
        queries_head, keys_head, values_head = triple
        scores = (
            jnp.einsum("fpd,gpd->pfg", queries_head, keys_head, preferred_element_type=jnp.float32)
            * score_scale
        )
        scores = jnp.where(causal[None], scores, MASKED)
        attention = softmax_rows(scores, 2)
        return jnp.einsum(
            "pfg,gpd->fpd", attention, values_head, preferred_element_type=jnp.float32
        ).astype(jnp.bfloat16)

    by_head = tuple(
        (jnp.moveaxis(array_in, 2, 0) for array_in in (queries, keys_block, values_block))
    )
    return jnp.moveaxis(lax.map(one_head, by_head), 0, 2)


def merge_stats(first_pair, second_pair):
    largest = jnp.maximum(first_pair[0], second_pair[0])
    totals = first_pair[1] * jnp.exp(first_pair[0] - largest) + second_pair[1] * jnp.exp(
        second_pair[0] - largest
    )
    return (largest, totals)


def local(
    frames_in, attn_gain, w_query, w_key, w_value, w_output, moe_gain, dispatch_keys, w_in, w_out
):
    frame_count, pos_count, features = frames_in.shape
    head_dim = features // HEADS
    normed = rms_scale(frames_in, attn_gain).astype(jnp.bfloat16)
    spread = lax.all_to_all(normed, "frame", split_axis=1, concat_axis=0, tiled=True)
    all_frames = spread.shape[0]
    pos_part = spread.shape[1]
    flattened = spread.reshape(all_frames * pos_part, features)
    shaped = (all_frames, pos_part, HEADS, head_dim)
    queries = project(flattened, w_query).reshape(shaped)
    keys_block = project(flattened, w_key).reshape(shaped)
    values_block = project(flattened, w_value).reshape(shaped)
    mixed_part = attend(queries, keys_block, values_block).reshape(all_frames, pos_part, features)
    mixed_heads = lax.all_to_all(mixed_part, "frame", split_axis=0, concat_axis=1, tiled=True)
    mixed_heads = mixed_heads.reshape(frame_count * pos_count, features)
    residual = (
        frames_in.reshape(frame_count * pos_count, features).astype(jnp.float32)
        + jnp.dot(mixed_heads, w_output, preferred_element_type=jnp.float32)
    ).astype(jnp.bfloat16)
    moe_input = rms_scale(residual, moe_gain).astype(jnp.bfloat16)
    logits = LOGIT_SCALE * jnp.dot(moe_input, dispatch_keys, preferred_element_type=jnp.float32)
    local_max = jnp.max(logits, axis=0)
    local_sum = jnp.sum(jnp.exp(logits - local_max[None, :]), axis=0)
    largest, totals = merged((local_max, local_sum), "pos", merge_stats)
    dispatch = (jnp.exp(logits - largest[None, :]) / totals[None, :]).astype(jnp.bfloat16)
    count_pos = lax.axis_size("pos")
    position = lax.axis_index("pos")
    splits = max(1, count_pos // EXPERTS)
    split_bits = splits.bit_length() - 1
    pieces_dev = EXPERTS * splits // count_pos
    local_experts = max(1, pieces_dev // splits)
    columns = dispatch
    slot_in = sum_at_owner(
        lax.dot_general(
            columns, moe_input, (((0,), (0,)), ((), ())), preferred_element_type=jnp.float32
        ).astype(jnp.bfloat16),
        "pos",
        0,
    ).astype(jnp.bfloat16)
    bit_index = 0
    partner = from_partner(slot_in, "pos", bit_index)
    upper_bit = position // 2**bit_index % 2 == 1
    slot_in = jnp.where(
        upper_bit,
        jnp.concatenate([partner, slot_in], axis=0),
        jnp.concatenate([slot_in, partner], axis=0),
    )
    slot_in = slot_in.reshape(local_experts, SLOTS, features)
    hidden = jax.nn.gelu(
        jnp.einsum("esd,edh->esh", slot_in, w_in, preferred_element_type=jnp.float32)
    ).astype(jnp.bfloat16)
    partial_out = jnp.einsum(
        "esh,ehd->esd", hidden, w_out, preferred_element_type=jnp.float32
    ).astype(jnp.bfloat16)
    shares = partial_out.astype(jnp.float32).reshape(pieces_dev * SLOTS, features)
    for bit_index in reversed(range(split_bits)):
        half_rows = shares.shape[0] // 2
        lower_half = shares[:half_rows]
        upper_half = shares[half_rows:]
        upper_bit = position // 2**bit_index % 2 == 1
        kept_rows = jnp.where(upper_bit, upper_half, lower_half)
        sent_rows = jnp.where(upper_bit, lower_half, upper_half)
        shares = kept_rows + from_partner(sent_rows.astype(jnp.bfloat16), "pos", bit_index).astype(
            sent_rows.dtype
        )
    outputs = shares.astype(jnp.bfloat16)
    combine = softmax_rows(logits, 1)
    columns = combine
    moe_out = jnp.dot(columns, collect(outputs, "pos", 0), preferred_element_type=jnp.float32)
    frames_out = (residual.astype(jnp.float32) + moe_out).astype(jnp.bfloat16)
    return frames_out.reshape(frame_count, pos_count, features)


def solution(mesh):
    in_specs = (
        P("frame", "pos", None),
        P(),
        P(),
        P(),
        P(),
        P(),
        P(),
        P(),
        P("pos", None, None),
        P("pos", None, None),
    )
    out_specs = P("frame", "pos", None)
    return jax.shard_map(local, mesh=mesh, in_specs=in_specs, out_specs=out_specs, check_vma=False)
```

profile of v0, /device:TPU:1, one launch (start us, length us, event | category | flops | bytes accessed | tf_op | source)
XLA Modules:
  0.0 160.5 jit_solution(891300015364039977)
XLA Ops:
  0.0 1.4 multiply_reduce_fusion
  1.5 2.1 %multiply_convert_fusion = bf16[64,8,512]{2,0,1:T(8,128)(2,1)} fusion(f32[512]{0:T(512)} %param.13, f32[64,8]{0,1:T(8,128)S(1)} %add_rsqrt_fusion, bf16[64,8,512]{2,1,0:T(8,128)(2,1)} %param.12), kind=kLoop, calls=%fused_computation.44 | loop fusion | flops 1048576 | bytes 1052672 | tf_op jit(solution)/shard_map/convert_element_type | solution.py:134
  3.5 6.0 %all-to-all-start = ((bf16[64,8,512]{2,0,1:T(8,128)(2,1)}), bf16[64,8,512]{2,0,1:T(8,128)(2,1)S(1)}, u32[]{:S(2)}, u32[]{:S(2)}) async-start(bf16[64,8,512]{2,0,1:T(8,128)(2,1)} %multiply_convert_fusion), calls=%async_computation | async-start | bytes 1048576 | tf_op jit(solution)/shard_map/all_to_all | solution.py:135
  9.5 8.7 %all-to-all-done = bf16[64,8,512]{2,0,1:T(8,128)(2,1)S(1)} async-done(((bf16[64,8,512]{2,0,1:T(8,128)(2,1)}), bf16[64,8,512]{2,0,1:T(8,128)(2,1)S(1)}, u32[]{:S(2)}, u32[]{:S(2)}) %all-to-all-start) | async-done | bytes 524320 | tf_op jit(solution)/shard_map/all_to_all | solution.py:135
  18.2 1.3 convolution_convert_fusion.3
  20.5 18.8 %while.11 = (s32[]{:T(128)}, bf16[8,512,1,64]{1,3,2,0:T(8,128)(2,1)}, bf16[8,512,1,64]{1,3,2,0:T(8,128)(2,1)S(1)}, bf16[8,512,1,64]{1,3,2,0:T(8,128)(2,1)}, bf16[8,512,1,64]{1,3,2,0:T(8,128)(2,1)S(1)}, /*index=5*/s32[]{:T(128)}) while((s32[]{:T(128)}, bf16[8,512,1,64]{1,3,2,0:T(8,128)(2,1)}, bf16[8,512,1,64]{1,3,2,0:T(8,128)(2,1)S(1)}, ...), condition=%wide.region_4.5_spmd.clone, body=%wide.region_1.4_spmd.clone.sunk | while | flops 69499904 | bytes 3420229 | solution.py:118
  20.5 1.2 fusion.86
  21.9 0.9 fusion.88
  22.9 1.2 fusion.86
  24.3 0.9 fusion.88
  25.2 1.2 fusion.86
  26.6 0.9 fusion.88
  27.6 1.2 fusion.86
  29.0 0.9 fusion.88
  29.9 1.2 fusion.86
  31.3 1.0 fusion.88
  32.3 1.2 fusion.86
  33.6 0.9 fusion.88
  34.6 1.2 fusion.86
  37.0 1.2 fusion.86
  39.8 2.0 %reduce.5 = bf16[512,512]{0,1:T(8,128)(2,1)S(1)} reduce(bf16[512,1,512]{0,2,1:T(8,128)(2,1)} %bitcast.117, bf16[]{:T(256)} %broadcast.50), dimensions={1}, to_apply=%copy.38.reduce_sub_computation | reduce | bytes 1048578 | tf_op jit(solution)/shard_map/reshape | solution.py:143
  42.1 1.2 reshape.156
  43.2 3.7 %all-to-all-start.1 = ((bf16[8,2,16384]{2,1,0:T(2,128)(2,1)}), bf16[8,2,16384]{2,1,0:T(2,128)(2,1)S(1)}, u32[]{:S(2)}, u32[]{:S(2)}) async-start(bf16[8,2,16384]{2,1,0:T(2,128)(2,1)} %reshape.156), calls=%async_computation.1 | async-start | bytes 1048576 | tf_op jit(solution)/shard_map/all_to_all | solution.py:144
  46.9 1.2 copy_convert_fusion
  48.1 6.9 %all-to-all-done.1 = bf16[8,2,16384]{2,1,0:T(2,128)(2,1)S(1)} async-done(((bf16[8,2,16384]{2,1,0:T(2,128)(2,1)}), bf16[8,2,16384]{2,1,0:T(2,128)(2,1)S(1)}, u32[]{:S(2)}, u32[]{:S(2)}) %all-to-all-start.1) | async-done | bytes 524320 | tf_op jit(solution)/shard_map/all_to_all | solution.py:144
  55.7 2.2 %fusion.20 = (f32[512]{0:T(512)S(1)}, bf16[512,512]{1,0:T(8,128)(2,1)S(1)}) fusion(bf16[512,512]{1,0:T(8,128)(2,1)S(1)} %copy-done.8, bf16[64,8,1,512]{3,0,1,2:T(8,128)(2,1)S(1)} %bitcast.116, f32[64,8,512]{2,0,1:T(8,128)} %copy_convert_fusion), kind=kOutput, calls=%fused_computation.38 | convolution fusion | flops 269745664 | bytes 2623488 | tf_op jit(solution)/shard_map/dot_general | solution.py:148
  59.7 26.0 %all_to_all.45 = f32[32,2,1024]{2,1,0:T(2,128)S(1)} all-to-all(f32[32,2,1024]{2,1,0:T(2,128)S(1)} %broadcast_in_dim.18), channel_id=1, replica_groups=mesh['frame'=8,'pos'=32] {'pos'}, dimensions={0} | all-to-all | bytes 524288 | tf_op jit(solution)/shard_map/all_to_all | solution.py:18
  86.5 1.9 %convolution_convert_fusion.1 = bf16[1024,512]{1,0:T(8,128)(2,1)S(1)} fusion(f32[512,1024]{1,0:T(8,128)S(1)} %get-tuple-element.80, f32[1024]{0:T(1024)S(1)} %bitcast.120, f32[1024]{0:T(1024)S(1)} %bitcast.121, bf16[512,512]{1,0:T(8,128)(2,1)} %copy-done.10, f32[512]{0:T(512)S(1)} %copy-done.9, f32[512]{0:T(512)S(1)} %add_rsqrt_fusion.1), kind=kOutput, calls=%fused_computation.27 | convolution fusion | flops 540016640 | bytes 3682304 | tf_op jit(solution)/shard_map/dot_general | solution.py:164
  88.4 32.1 %all_to_all.46 = bf16[32,32,512]{2,1,0:T(8,128)(2,1)S(1)} all-to-all(bf16[32,32,512]{2,1,0:T(8,128)(2,1)S(1)} %bitcast.112), channel_id=1, replica_groups=mesh['frame'=8,'pos'=32] {'pos'}, dimensions={0} | all-to-all | bytes 2097152 | tf_op jit(solution)/shard_map/all_to_all | solution.py:58
  122.4 1.7 %fusion.19 = f32[1,64,512]{2,1,0:T(8,128)S(1)} fusion(bf16[1,1024,512]{2,1,0:T(8,128)(2,1)S(1)} %copy-done.4, bf16[1,512,1024]{2,1,0:T(8,128)(2,1)} %param.20, bf16[32,512]{1,0:T(8,128)(2,1)S(1)} %reduce_sum.61, bf16[32,512]{1,0:T(8,128)(2,1)S(1)} %collective-permute-done, pred[]{:T(512)S(6)} %eq.7), kind=kOutput, calls=%fused_computation.37 | convolution fusion | flops 135168000 | bytes 2293761 | tf_op jit(solution)/shard_map/esh,ehd->esd/dot_general | solution.py:182
  125.6 33.3 %all_to_all.47 = bf16[32,32,512]{2,1,0:T(8,128)(2,1)S(1)} all-to-all(bf16[32,32,512]{2,1,0:T(8,128)(2,1)S(1)} %broadcast_in_dim.19), channel_id=1, replica_groups=mesh['frame'=8,'pos'=32] {'pos'}, dimensions={0} | all-to-all | bytes 2097152 | tf_op jit(solution)/shard_map/all_to_all | solution.py:18
  158.9 1.6 fusion.17
  (78 shorter events, 11.6 us)
Async XLA Ops:
  0.0 58.0 %copy-start = (bf16[512,1024]{1,0:T(8,128)(2,1)S(1)}, bf16[512,1024]{1,0:T(8,128)(2,1)}, u32[]{:S(2)}) copy-start(bf16[512,1024]{1,0:T(8,128)(2,1)} %param.19) | copy-start | bytes 3145732
  0.0 18.2 %copy-start.5 = (bf16[512,512]{1,0:T(8,128)(2,1)S(1)}, bf16[512,512]{1,0:T(8,128)(2,1)}, u32[]{:S(2)}) copy-start(bf16[512,512]{1,0:T(8,128)(2,1)} %param.14) | copy-start | bytes 1572868
  0.0 19.5 %copy-start.6 = (bf16[512,512]{1,0:T(8,128)(2,1)S(1)}, bf16[512,512]{1,0:T(8,128)(2,1)}, u32[]{:S(2)}) copy-start(bf16[512,512]{1,0:T(8,128)(2,1)} %param.15) | copy-start | bytes 1572868
  3.5 16.5 %copy-start.7 = (bf16[512,512]{1,0:T(8,128)(2,1)S(1)}, bf16[512,512]{1,0:T(8,128)(2,1)}, u32[]{:S(2)}) copy-start(bf16[512,512]{1,0:T(8,128)(2,1)} %param.16) | copy-start | bytes 1572868
  3.5 14.7 %all-to-all-start = ((bf16[64,8,512]{2,0,1:T(8,128)(2,1)}), bf16[64,8,512]{2,0,1:T(8,128)(2,1)S(1)}, u32[]{:S(2)}, u32[]{:S(2)}) async-start(bf16[64,8,512]{2,0,1:T(8,128)(2,1)} %multiply_convert_fusion), calls=%async_computation | async-start | bytes 1048576 | tf_op jit(solution)/shard_map/all_to_all | solution.py:135
  39.8 7.1 %copy-start.1 = (bf16[64,8,512]{2,1,0:T(8,128)(2,1)S(1)}, bf16[64,8,512]{2,1,0:T(8,128)(2,1)}, u32[]{:S(2)}) copy-start(bf16[64,8,512]{2,1,0:T(8,128)(2,1)} %param.12) | copy-start | bytes 1572868
  43.2 11.8 %all-to-all-start.1 = ((bf16[8,2,16384]{2,1,0:T(2,128)(2,1)}), bf16[8,2,16384]{2,1,0:T(2,128)(2,1)S(1)}, u32[]{:S(2)}, u32[]{:S(2)}) async-start(bf16[8,2,16384]{2,1,0:T(2,128)(2,1)} %reshape.156), calls=%async_computation.1 | async-start | bytes 1048576 | tf_op jit(solution)/shard_map/all_to_all | solution.py:144
  48.1 7.6 %copy-start.8 = (bf16[512,512]{1,0:T(8,128)(2,1)S(1)}, bf16[512,512]{1,0:T(8,128)(2,1)}, u32[]{:S(2)}) copy-start(bf16[512,512]{1,0:T(8,128)(2,1)} %param.17) | copy-start | bytes 1572868
  55.6 2.4 %copy-start.9 = (f32[512]{0:T(512)S(1)}, f32[512]{0:T(512)}, u32[]{:S(2)}) copy-start(f32[512]{0:T(512)} %param.18) | copy-start | bytes 6148
  57.9 0.9 copy-start.10
  58.9 27.7 %copy-start.2 = (f32[512,1024]{1,0:T(8,128)}, f32[512,1024]{1,0:T(8,128)S(1)}, u32[]{:S(2)}) copy-start(f32[512,1024]{1,0:T(8,128)S(1)} %get-tuple-element.80) | copy-start | bytes 6291460
  88.4 34.0 %copy-start.4 = (bf16[1,1024,512]{2,1,0:T(8,128)(2,1)S(1)}, bf16[1,1024,512]{2,1,0:T(8,128)(2,1)}, u32[]{:S(2)}) copy-start(bf16[1,1024,512]{2,1,0:T(8,128)(2,1)} %param.21) | copy-start | bytes 3145732
  120.7 1.7 %collective-permute-start = (bf16[32,512]{1,0:T(8,128)(2,1)S(1)}, bf16[32,512]{1,0:T(8,128)(2,1)S(1)}, u32[]{:S(2)}, u32[]{:S(2)}) collective-permute-start(bf16[32,512]{1,0:T(8,128)(2,1)S(1)} %reduce_sum.61), channel_id=1, source_target_pairs={{0,1},{1,0},{2,3},{3,2},{4,5},{5,4},{6,7},{7,6},{8,9},{9,8},{10,11... | collective-permute-start | bytes 98312 | tf_op jit(solution)/shard_map/ppermute | solution.py:69
  124.1 34.8 %copy-start.3 = (f32[512,1024]{1,0:T(8,128)S(1)}, f32[512,1024]{1,0:T(8,128)}, u32[]{:S(2)}) copy-start(f32[512,1024]{1,0:T(8,128)} %copy-done.2) | copy-start | bytes 6291460
  124.2 34.8 %copy-start.11 = (bf16[512,512]{1,0:T(8,128)(2,1)S(1)}, bf16[512,512]{1,0:T(8,128)(2,1)}, u32[]{:S(2)}) copy-start(bf16[512,512]{1,0:T(8,128)(2,1)} %copy-done.10) | copy-start | bytes 1572868
  124.2 1.3 collective-permute-start.1
where the time goes:
time: 161 us
  blocking collectives  91.4 us (57%)
  matrix products  27.7 us (17%)
  waiting for transfers between devices  17.4 us (11%)
  starting transfers between devices  10.9 us (7%)
  other arithmetic  9.34 us (6%)
  local copies, waits for them, and re-layouts  3.4 us (2%)
    all_to_all x2, blocking collectives, copy_for_each(): return lax.all_to_all(copies, axis, split_axis=0, concat_axis=0, tiled=True)  59.3 us
    all_to_all x1, blocking collectives, sum_at_owner(): lax.all_to_all(in_blocks(shard, dim, length), axis, 0, 0, tiled=True)  32.1 us
    dot_general x8, matrix products, one_head(): jnp.einsum('fpd,gpd->pfg', queries_head, keys_head, preferred_element_typ...  9.6 us
    all_to_all x1, waiting for transfers between devices, local(): lax.all_to_all(normed, 'frame', split_axis=1, concat_axis=0, tiled=True)  8.71 us
    dot_general x8, matrix products, one_head(): jnp.einsum('pfg,gpd->fpd', attention, values_head, preferred_element_type...  7.6 us
    all_to_all x1, waiting for transfers between devices, local(): lax.all_to_all(mixed_part, 'frame', split_axis=0, concat_axis=1, tiled=True)  6.94 us
    all_to_all x1, starting transfers between devices, local(): lax.all_to_all(normed, 'frame', split_axis=1, concat_axis=0, tiled=True)  5.98 us
    all_to_all x1, starting transfers between devices, local(): lax.all_to_all(mixed_part, 'frame', split_axis=0, concat_axis=1, tiled=True)  3.67 us
  transfers between devices with their start and end apart: 4, of which 4 were waited for; matrix products, arithmetic and copies ran while one was open for 1% of the time, Pallas kernels for 0%

commit v1 on v0

v1 whole, which is shorter than its diff:
```python
import jax
import jax.numpy as jnp
from jax import lax
from jax.experimental import pallas as pl
from jax.experimental.pallas import tpu as pltpu
from jax.sharding import PartitionSpec as P

HEADS = 8
EXPERTS = 16
SLOTS = 64

EPS = 1e-06
LOGIT_SCALE = 3.0
MASKED = -1e30
LOG2E = 1.4426950408889634

F32 = jnp.float32
BF16 = jnp.bfloat16
VMEM = pl.BlockSpec(memory_space=pltpu.VMEM)
STAT_ROWS = 8


def nn(a, b):
    return lax.dot_general(a, b, (((1,), (0,)), ((), ())), preferred_element_type=F32)


def nt(a, b):
    return lax.dot_general(a, b, (((1,), (1,)), ((), ())), preferred_element_type=F32)


def call(kernel, out_shape, args, scratch=(), flops=1 << 20, transcendentals=0):
    single = isinstance(out_shape, jax.ShapeDtypeStruct)
    outs = (out_shape,) if single else tuple(out_shape)
    moved = sum(a.size * a.dtype.itemsize for a in (*args, *outs))
    return pl.pallas_call(
        kernel,
        out_shape=out_shape,
        in_specs=[VMEM] * len(args),
        out_specs=VMEM if single else tuple([VMEM] * len(outs)),
        scratch_shapes=list(scratch),
        cost_estimate=pl.CostEstimate(
            flops=flops, bytes_accessed=moved, transcendentals=transcendentals
        ),
    )(*args)


def one_hot(rows, outer, inner):
    row = lax.broadcasted_iota(jnp.int32, (rows, rows), 0)
    col = lax.broadcasted_iota(jnp.int32, (rows, rows), 1)
    source = (row & (inner - 1)) * outer + lax.shift_right_logical(row, inner.bit_length() - 1)
    return jnp.where(col == source, 1.0, 0.0).astype(BF16)


def by_position_kernel(frames, positions, x_ref, o_ref):
    rows = frames * positions
    o_ref[...] = nn(one_hot(rows, positions, frames), x_ref[...]).astype(BF16)


def rms(rows, gain):
    mean_sq = jnp.mean(rows * rows, axis=-1, keepdims=True)
    return (rows * lax.rsqrt(mean_sq + EPS) * gain).astype(BF16)


def attention_kernel(x_ref, gain_ref, wq_ref, wk_ref, wv_ref, o_ref, n_s, q_s, k_s, v_s):
    frames, features = x_ref.shape
    n_s[...] = rms(x_ref[...].astype(F32), gain_ref[...])
    q_s[...] = nn(n_s[...], wq_ref[...]).astype(BF16)
    k_s[...] = nn(n_s[...], wk_ref[...]).astype(BF16)
    v_s[...] = nn(n_s[...], wv_ref[...]).astype(BF16)
    head_dim = features // HEADS
    scale = head_dim ** (-0.5) * LOG2E
    block = 256
    row = lax.broadcasted_iota(jnp.int32, (block, block), 0)
    col = lax.broadcasted_iota(jnp.int32, (block, block), 1)
    causal = row >= col
    low = lax.broadcasted_iota(jnp.int32, (1, 128), 1) < head_dim
    for pair in range(features // 128):
        lanes = slice(pair * 128, pair * 128 + 128)
        for start in range(0, frames, block):
            count = start + block
            mixed = []
            for mine in (low, jnp.logical_not(low)):
                q = jnp.where(mine, q_s[start:count, lanes], jnp.zeros((), BF16))
                t = nt(q, k_s[:count, lanes]) * scale
                last = jnp.where(causal, t[:, start:], MASKED)
                t = last if start == 0 else jnp.concatenate([t[:, :start], last], axis=1)
                weights = jnp.exp2(t - jnp.max(t, axis=1, keepdims=True)).astype(BF16)
                v = jnp.where(mine, v_s[:count, lanes], jnp.ones((), BF16))
                both = nn(weights, v)
                mixed.append(both / pltpu.roll(both, head_dim, 1))
            o_ref[start:count, lanes] = jnp.where(low, mixed[0], mixed[1]).astype(BF16)


def residual_kernel(mixed_ref, x_ref, wo_ref, gain_ref, r_ref, m_ref):
    r = (x_ref[...].astype(F32) + nn(mixed_ref[...], wo_ref[...])).astype(BF16)
    r_ref[...] = r
    m_ref[...] = rms(r.astype(F32), gain_ref[...])


def combine_kernel(m_ref, keys_ref, c_ref):
    rows = 128
    for start in range(0, m_ref.shape[0], rows):
        part = slice(start, start + rows)
        t = nn(m_ref[part, :], keys_ref[...]) * (LOGIT_SCALE * LOG2E)
        w = jnp.exp2(t - jnp.max(t, axis=1, keepdims=True))
        c_ref[part, :] = (w / jnp.sum(w, axis=1, keepdims=True)).astype(BF16)


def dispatch_kernel(m_ref, other_ref, keys_ref, o_ref, all_s):
    tokens, features = m_ref.shape
    all_s[:tokens, :] = m_ref[...]
    all_s[tokens:, :] = other_ref[...]
    half = SLOTS // 2
    for start in range(0, keys_ref.shape[0], 128):
        t = nt(keys_ref[start : start + 128, :], all_s[...]) * (LOGIT_SCALE * LOG2E)
        largest = jnp.max(t, axis=1, keepdims=True)
        w = jnp.exp2(t - largest)
        total = jnp.sum(w, axis=1, keepdims=True)
        sums = (nn(w.astype(BF16), all_s[...]) / total).astype(BF16)
        lse = jnp.broadcast_to(largest + jnp.log2(total), (128, 128)).T[:STAT_ROWS, :]
        high = lse.astype(BF16).astype(F32)
        middle = (lse - high).astype(BF16).astype(F32)
        rest = lse - high - middle
        line = lax.broadcasted_iota(jnp.int32, lse.shape, 0)
        stats = jnp.where(
            line == 0, high, jnp.where(line == 1, middle, jnp.where(line == 2, rest, 0.0))
        ).astype(BF16)
        for k in range(128 // half):
            expert = start // half + k
            for j in range(features // 128):
                o_ref[expert, j * half : (j + 1) * half, :] = sums[
                    k * half : (k + 1) * half, j * 128 : (j + 1) * 128
                ]
            o_ref[expert, features // 128 * half :, :] = stats


def merge_kernel(got_ref, o_ref, w_s):
    chips = got_ref.shape[0]
    half = SLOTS // 2
    tall = o_ref.shape[1] // 128 * half
    lse = jnp.concatenate(
        [
            jnp.sum(got_ref[s, tall:, :].astype(F32), axis=0, keepdims=True)
            for s in range(chips)
        ],
        axis=0,
    )
    w = jnp.exp2(lse - jnp.max(lse, axis=0, keepdims=True))
    w = w / jnp.sum(w, axis=0, keepdims=True)
    w_s[...] = jnp.concatenate([w, jnp.zeros((128 - chips, 128), F32)], axis=0).T
    place = lax.rem(lax.axis_index("pos") // 2, 128 // half)
    mine = w_s[pl.ds(pl.multiple_of(place * half, half), half), :]
    for j in range(o_ref.shape[1] // 128):
        total = jnp.zeros((half, 128), F32)
        for s in range(chips):
            total += mine[:, s : s + 1] * got_ref[s, j * half : (j + 1) * half, :].astype(F32)
        o_ref[:, j * 128 : (j + 1) * 128] = total.astype(BF16)


def expert_kernel(own_ref, other_ref, w_in_ref, w_out_ref, own_out, other_out):
    half = own_ref.shape[0]
    rows = jnp.concatenate([own_ref[...], other_ref[...]], axis=0)
    hidden = jax.nn.gelu(nn(rows, w_in_ref[...])).astype(BF16)
    out = nn(hidden, w_out_ref[...]).astype(BF16)
    own_out[...] = out[:half, :]
    other_out[...] = out[half:, :]


def output_kernel(frames, positions, r_ref, c_ref, own_ref, other_ref, o_ref, all_s):
    half = SLOTS // 2
    core = lax.rem(lax.axis_index("pos"), 2)
    for e in range(EXPERTS):
        part = slice(e * half, (e + 1) * half)
        at = pl.multiple_of(e * SLOTS + core * half, half)
        all_s[pl.ds(at, half), :] = own_ref[part, :]
        at = pl.multiple_of(e * SLOTS + (1 - core) * half, half)
        all_s[pl.ds(at, half), :] = other_ref[part, :]
    out = (r_ref[...].astype(F32) + nn(c_ref[...], all_s[...])).astype(BF16)
    o_ref[...] = nn(one_hot(frames * positions, frames, positions), out).astype(BF16)


def from_other_core(block):
    return lax.ppermute(block, "pos", [(k, k ^ 1) for k in range(lax.axis_size("pos"))])


def local(
    frames_in, attn_gain, w_query, w_key, w_value, w_output, moe_gain, dispatch_keys, w_in, w_out
):
    frame_count, pos_count, features = frames_in.shape
    tokens = frame_count * pos_count
    chips = lax.axis_size("pos") // 2
    half = SLOTS // 2
    by_core = [[2 * chip + core for chip in range(chips)] for core in range(2)]
    wide = jax.ShapeDtypeStruct((tokens, features), BF16)

    def by_position(x_ref, o_ref):
        by_position_kernel(frame_count, pos_count, x_ref, o_ref)

    def output(*refs):
        output_kernel(frame_count, pos_count, *refs)

    x = call(by_position, wide, (frames_in.reshape(tokens, features),), flops=2 * tokens**2 * features)
    spread = lax.all_to_all(
        x.reshape(pos_count, frame_count, features), "frame", split_axis=0, concat_axis=0, tiled=True
    )
    core = lax.rem(lax.axis_index("pos"), 2)
    by_half = dispatch_keys.T.reshape(EXPERTS, 2, half, features)
    half_keys = lax.dynamic_index_in_dim(by_half, core, 1, keepdims=False).reshape(-1, features)

    mixed = call(
        attention_kernel,
        wide,
        (spread.reshape(tokens, features), attn_gain.reshape(1, -1), w_query, w_key, w_value),
        scratch=[pltpu.VMEM((tokens, features), BF16)] * 4,
        flops=14 * tokens**2 * features,
        transcendentals=HEADS * tokens**2,
    )
    mixed = lax.all_to_all(
        mixed.reshape(pos_count, frame_count, features),
        "frame",
        split_axis=0,
        concat_axis=0,
        tiled=True,
    )
    residual, moe_input = call(
        residual_kernel,
        (wide, wide),
        (mixed.reshape(tokens, features), x, w_output, moe_gain.reshape(1, -1)),
        flops=2 * tokens**2 * features,
    )
    other_input = from_other_core(moe_input)
    combine = call(
        combine_kernel,
        jax.ShapeDtypeStruct((tokens, EXPERTS * SLOTS), BF16),
        (moe_input, dispatch_keys),
        flops=4 * tokens**2 * features,
        transcendentals=2 * tokens**2,
    )
    sums = call(
        dispatch_kernel,
        jax.ShapeDtypeStruct((chips, features // 128 * half + STAT_ROWS, 128), BF16),
        (moe_input, other_input, half_keys),
        scratch=[pltpu.VMEM((2 * tokens, features), BF16)],
        flops=8 * tokens**2 * features,
        transcendentals=2 * tokens**2,
    )
    sums = lax.all_to_all(
        sums, "pos", split_axis=0, concat_axis=0, tiled=True, axis_index_groups=by_core
    )
    narrow = jax.ShapeDtypeStruct((half, features), BF16)
    slot_in = call(merge_kernel, narrow, (sums,), scratch=[pltpu.VMEM((128, 128), F32)])
    other_slots = from_other_core(slot_in)
    own_part, other_part = call(
        expert_kernel,
        (narrow, narrow),
        (slot_in, other_slots, w_in[0], w_out[0]),
        flops=8 * SLOTS * features**2,
    )
    outputs = (own_part.astype(F32) + from_other_core(other_part).astype(F32)).astype(BF16)
    own_half = lax.all_to_all(
        jnp.broadcast_to(outputs, (chips, *outputs.shape)),
        "pos",
        split_axis=0,
        concat_axis=0,
        tiled=True,
        axis_index_groups=by_core,
    ).reshape(-1, features)
    other_half = from_other_core(own_half)
    out = call(
        output,
        wide,
        (residual, combine, own_half, other_half),
        scratch=[pltpu.VMEM((EXPERTS * SLOTS, features), BF16)],
        flops=6 * tokens**2 * features,
    )
    return out.reshape(frame_count, pos_count, features)


def solution(mesh):
    in_specs = (
        P("frame", "pos", None),
        P(),
        P(),
        P(),
        P(),
        P(),
        P(),
        P(),
        P("pos", None, None),
        P("pos", None, None),
    )
    out_specs = P("frame", "pos", None)
    return jax.shard_map(local, mesh=mesh, in_specs=in_specs, out_specs=out_specs, check_vma=False)
```

time: 161 us -> 122 us (0.76)
  Pallas kernels: 0 us -> 29.6 us
  matrix products: 27.7 us -> 0 us
  waiting for transfers between devices: 17.4 us -> 2.48 us
  blocking collectives: 91.4 us -> 76.5 us
  other arithmetic: 9.34 us -> 0.77 us
  starting transfers between devices: 10.9 us -> 8.47 us
    pallas_call x0 -> x8, Pallas kernels: none -> 29.6 us  [call(): pl.pallas_call(kernel, out_shape=out_shape, in_specs=[VMEM] * len(args),...]
    dot_general x24 -> x0, matrix products: 27.7 us -> none  [the longest x8 9.6 us: one_head(): jnp.einsum('fpd,gpd->pfg', queries_head, keys_head, preferred_element_typ...]
    all_to_all x2 -> x0, waiting for transfers between devices: 15.7 us -> none  [the longest x1 8.71 us: local(): lax.all_to_all(normed, 'frame', split_axis=1, concat_axis=0, tiled=True)]
    all_to_all x3 -> x4, blocking collectives: 91.4 us -> 76.5 us  [the longest x1 30.6 us: local(): lax.all_to_all(sums, 'pos', split_axis=0, concat_axis=0, tiled=True, axis...]
    all_to_all x2 -> x0, starting transfers between devices: 9.66 us -> none  [the longest x1 5.98 us: local(): lax.all_to_all(normed, 'frame', split_axis=1, concat_axis=0, tiled=True)]
    ppermute x2 -> x4, starting transfers between devices: 1.26 us -> 8.47 us  [from_other_core(): lax.ppermute(block, 'pos', [(k, k ^ 1) for k in range(lax.axis_size('pos'...]
    reduce_sum x11 -> x0, other arithmetic: 3.9 us -> none  [the longest x9 2.31 us: softmax_rows(): jnp.sum(weights, axis=axis_index, keepdims=True)]
    convert_element_type x4 -> x1, other arithmetic: 3.25 us -> 0.77 us  [local(): (own_part.astype(F32) + from_other_core(other_part).astype(F32)).astype(B...]
  transfers between devices with their start and end apart: 4 -> 4, of which waited for: 4 -> 3; matrix products, arithmetic and copies ran while one was open for 1% -> 1% of each run, Pallas kernels for 0% -> 3%
where the time goes in v1:
time: 122 us; the launch traced here: 121 us
  blocking collectives  76.5 us (63%)
  Pallas kernels  29.6 us (24%)
  starting transfers between devices  8.47 us (7%)
  local copies, waits for them, and re-layouts  3.63 us (3%)
  waiting for transfers between devices  2.48 us (2%)
    all_to_all x1, blocking collectives, local(): lax.all_to_all(sums, 'pos', split_axis=0, concat_axis=0, tiled=True, axis...  30.6 us
    pallas_call x8, Pallas kernels, call(): pl.pallas_call(kernel, out_shape=out_shape, in_specs=[VMEM] * len(args),...  29.6 us
    all_to_all x1, blocking collectives, local(): lax.all_to_all(jnp.broadcast_to(outputs, (chips, *outputs.shape)), 'pos',...  20.3 us
    all_to_all x1, blocking collectives, local(): lax.all_to_all(x.reshape(pos_count, frame_count, features), 'frame', spli...  14.2 us
    all_to_all x1, blocking collectives, local(): lax.all_to_all(mixed.reshape(pos_count, frame_count, features), 'frame',...  11.4 us
    ppermute x4, starting transfers between devices, from_other_core(): lax.ppermute(block, 'pos', [(k, k ^ 1) for k in range(lax.axis_size('pos'...  8.47 us
    unnamed x11, local copies, waits for them, and re-layouts  2.73 us
    ppermute x4, waiting for transfers between devices, from_other_core(): lax.ppermute(block, 'pos', [(k, k ^ 1) for k in range(lax.axis_size('pos'...  2.48 us
  transfers between devices with their start and end apart: 4, of which 3 were waited for; matrix products, arithmetic and copies ran while one was open for 1% of the time, Pallas kernels for 3%

profile of v1, /device:TPU:1, one launch (start us, length us, event | category | flops | bytes accessed | tf_op | source)
XLA Modules:
  0.0 121.4 jit_solution(9263093697027100762)
XLA Ops:
  0.0 2.3 %shard_map.100.x_ref = bf16[512,512]{1,0:T(8,128)(2,1)} custom-call(bf16[512,512]{1,0:T(8,128)(2,1)} %bitcast.22), custom_call_target="tpu_custom_call" | custom-call | flops 268435456 | bytes 1048576 | tf_op jit(solution)/shard_map/pallas_call | solution.py:35
  2.3 14.2 %all_to_all.20 = bf16[8,64,512]{2,1,0:T(8,128)(2,1)} all-to-all(bf16[8,64,512]{2,1,0:T(8,128)(2,1)} %bitcast.15), channel_id=1, replica_groups=mesh['frame'=8,'pos'=32] {'frame'}, dimensions={0} | all-to-all | bytes 1048576 | tf_op jit(solution)/shard_map/all_to_all | solution.py:203
  16.5 7.6 %shard_map.101 = bf16[512,512]{1,0:T(8,128)(2,1)} custom-call(bf16[512,512]{1,0:T(8,128)(2,1)} %bitcast.24, f32[1,512]{1,0:T(1,128)} %bitcast.27, bf16[512,512]{1,0:T(8,128)(2,1)} %wq_ref.1, bf16[512,512]{1,0:T(8,128)(2,1)} %wk_ref.1, bf16[512,512]{1,0:T(8,128)(2,1)} %wv_ref.1), custom_call_target="tpu_custom_call" | custom-call | flops 1879048192 | bytes 2623488 | tf_op jit(solution)/shard_map/pallas_call | solution.py:35
  24.0 11.4 %all_to_all.21 = bf16[8,64,512]{2,1,0:T(8,128)(2,1)} all-to-all(bf16[8,64,512]{2,1,0:T(8,128)(2,1)} %bitcast.23), channel_id=1, replica_groups=mesh['frame'=8,'pos'=32] {'frame'}, dimensions={0} | all-to-all | bytes 1048576 | tf_op jit(solution)/shard_map/all_to_all | solution.py:218
  35.4 0.0 copy-start
  35.4 2.9 %shard_map.102 = (bf16[512,512]{1,0:T(8,128)(2,1)}, bf16[512,512]{1,0:T(8,128)(2,1)}) custom-call(bf16[512,512]{1,0:T(8,128)(2,1)} %bitcast.17, bf16[512,512]{1,0:T(8,128)(2,1)} %shard_map.100.x_ref, bf16[512,512]{1,0:T(8,128)(2,1)} %wo_ref.1, f32[1,512]{1,0:T(1,128)} %bitcast.26), custom_call_target="tpu_custom_call" | custom-call | flops 268435456 | bytes 2623488 | tf_op jit(solution)/shard_map/pallas_call | solution.py:35
  38.3 3.7 %collective-permute-start = (bf16[512,512]{1,0:T(8,128)(2,1)}, bf16[512,512]{1,0:T(8,128)(2,1)S(1)}, u32[]{:S(2)}, u32[]{:S(2)}) collective-permute-start(bf16[512,512]{1,0:T(8,128)(2,1)} %get-tuple-element.10.m_ref), channel_id=1, source_target_pairs={{0,1},{1,0},{2,3},{3,2},{4,5},{5,4},{6,7},{7,6},{8,9},{9,8},{10,11... | collective-permute-start | bytes 1572872 | tf_op jit(solution)/shard_map/ppermute | solution.py:183
  42.1 0.0 copy-done
  42.1 0.5 copy.12
  42.6 0.9 constant_dynamic-slice_fusion
  43.5 0.3 collective-permute-done.other_ref
  43.8 0.0 copy-start.4
  43.8 0.8 copy-done.4
  44.6 5.1 %shard_map.104 = bf16[16,136,128]{2,1,0:T(8,128)(2,1)} custom-call(bf16[512,512]{1,0:T(8,128)(2,1)} %get-tuple-element.10.m_ref, bf16[512,512]{1,0:T(8,128)(2,1)} %copy-done.4, bf16[512,512]{1,0:T(8,128)(2,1)} %bitcast.25), custom_call_target="tpu_custom_call" | custom-call | flops 1073741824 | bytes 2129920 | tf_op jit(solution)/shard_map/pallas_call | solution.py:35
  49.7 30.6 %all_to_all.22.got_ref = bf16[16,136,128]{2,1,0:T(8,128)(2,1)} all-to-all(bf16[16,136,128]{2,1,0:T(8,128)(2,1)} %shard_map.104), channel_id=1, replica_groups={{0,2,4,6,8,10,12,14,16,18,20,22,24,26,28,30},{1,3,5,7,9,11,13,15,17,19,..., dimensions={0} | all-to-all | bytes 1114112 | tf_op jit(solution)/shard_map/all_to_all | solution.py:247
  80.2 2.0 %shard_map.105.own_ref = bf16[32,512]{1,0:T(8,128)(2,1)} custom-call(bf16[16,136,128]{2,1,0:T(8,128)(2,1)} %all_to_all.22.got_ref), custom_call_target="tpu_custom_call" | custom-call | flops 1048576 | bytes 589824 | tf_op jit(solution)/shard_map/pallas_call | solution.py:35
  82.3 1.7 %collective-permute-start.1 = (bf16[32,512]{1,0:T(8,128)(2,1)}, bf16[32,512]{1,0:T(8,128)(2,1)S(1)}, u32[]{:S(2)}, u32[]{:S(2)}) collective-permute-start(bf16[32,512]{1,0:T(8,128)(2,1)} %shard_map.105.own_ref), channel_id=1, source_target_pairs={{0,1},{1,0},{2,3},{3,2},{4,5},{5,4},{6,7},{7,6},{8,9},{9,8},{10,11... | collective-permute-start | bytes 98312 | tf_op jit(solution)/shard_map/ppermute | solution.py:183
  84.0 1.1 collective-permute-done.1.other_ref
  85.0 0.0 copy-start.3
  85.0 0.6 copy-done.3
  85.6 2.7 %shard_map.106 = (bf16[32,512]{1,0:T(8,128)(2,1)}, bf16[32,512]{1,0:T(8,128)(2,1)}) custom-call(bf16[32,512]{1,0:T(8,128)(2,1)} %shard_map.105.own_ref, bf16[32,512]{1,0:T(8,128)(2,1)} %copy-done.3, bf16[512,1024]{1,0:T(8,128)(2,1)} %bitcast.20, bf16[1024,512]{1,0:T(8,128)(2,1)} %bitcast.21), custom_call_target="tpu_custom_call" | custom-call | flops 134217728 | bytes 2228224 | tf_op jit(solution)/shard_map/pallas_call | solution.py:35
  88.4 0.3 collective-permute-start.2
  88.7 1.1 collective-permute-done.2
  89.8 0.8 add_convert_fusion
  90.6 20.3 %all_to_all.23 = bf16[16,32,512]{2,1,0:T(8,128)(2,1)S(1)} all-to-all(bf16[16,32,512]{2,1,0:T(8,128)(2,1)S(1)} %broadcast_in_dim.3), channel_id=1, replica_groups={{0,2,4,6,8,10,12,14,16,18,20,22,24,26,28,30},{1,3,5,7,9,11,13,15,17,19,..., dimensions={0} | all-to-all | bytes 1048576 | tf_op jit(solution)/shard_map/all_to_all | solution.py:260
  110.9 0.0 copy-start.1
  110.9 2.7 %collective-permute-start.3 = (bf16[512,512]{1,0:T(8,128)(2,1)S(1)}, bf16[512,512]{1,0:T(8,128)(2,1)S(1)}, u32[]{:S(2)}, u32[]{:S(2)}) collective-permute-start(bf16[512,512]{1,0:T(8,128)(2,1)S(1)} %bitcast.18), channel_id=1, source_target_pairs={{0,1},{1,0},{2,3},{3,2},{4,5},{5,4},{6,7},{7,6},{8,9},{9,8},{10,11... | collective-permute-start | bytes 1572872 | tf_op jit(solution)/shard_map/ppermute | solution.py:183
  113.6 3.5 %shard_map.103.refs_1_ = bf16[512,1024]{1,0:T(8,128)(2,1)} custom-call(bf16[512,512]{1,0:T(8,128)(2,1)} %get-tuple-element.10.m_ref, bf16[512,1024]{1,0:T(8,128)(2,1)} %keys_ref.1), custom_call_target="tpu_custom_call" | custom-call | flops 536870912 | bytes 2621440 | tf_op jit(solution)/shard_map/pallas_call | solution.py:35
  117.1 0.0 copy-done.1
  117.1 0.0 collective-permute-done.3.refs_3_
  117.1 0.8 copy-done.2
  117.9 3.6 %shard_map.107 = bf16[512,512]{1,0:T(8,128)(2,1)} custom-call(bf16[512,512]{1,0:T(8,128)(2,1)} %get-tuple-element.9.refs_0_, bf16[512,1024]{1,0:T(8,128)(2,1)} %shard_map.103.refs_1_, bf16[512,512]{1,0:T(8,128)(2,1)} %bitcast.19, bf16[512,512]{1,0:T(8,128)(2,1)} %copy-done.2), custom_call_target="tpu_custom_call" | custom-call | flops 805306368 | bytes 3145728 | tf_op jit(solution)/shard_map/pallas_call | solution.py:35
  (2 shorter events, 0.0 us)
Async XLA Ops:
  35.4 6.6 %copy-start = (bf16[512,1024]{1,0:T(8,128)(2,1)S(1)}, bf16[512,1024]{1,0:T(8,128)(2,1)}, u32[]{:S(2)}) copy-start(bf16[512,1024]{1,0:T(8,128)(2,1)} %keys_ref.1) | copy-start | bytes 3145732
  38.3 5.5 %collective-permute-start = (bf16[512,512]{1,0:T(8,128)(2,1)}, bf16[512,512]{1,0:T(8,128)(2,1)S(1)}, u32[]{:S(2)}, u32[]{:S(2)}) collective-permute-start(bf16[512,512]{1,0:T(8,128)(2,1)} %get-tuple-element.10.m_ref), channel_id=1, source_target_pairs={{0,1},{1,0},{2,3},{3,2},{4,5},{5,4},{6,7},{7,6},{8,9},{9,8},{10,11... | collective-permute-start | bytes 1572872 | tf_op jit(solution)/shard_map/ppermute | solution.py:183
  43.8 0.8 copy-start.4
  82.3 2.8 %collective-permute-start.1 = (bf16[32,512]{1,0:T(8,128)(2,1)}, bf16[32,512]{1,0:T(8,128)(2,1)S(1)}, u32[]{:S(2)}, u32[]{:S(2)}) collective-permute-start(bf16[32,512]{1,0:T(8,128)(2,1)} %shard_map.105.own_ref), channel_id=1, source_target_pairs={{0,1},{1,0},{2,3},{3,2},{4,5},{5,4},{6,7},{7,6},{8,9},{9,8},{10,11... | collective-permute-start | bytes 98312 | tf_op jit(solution)/shard_map/ppermute | solution.py:183
  85.0 0.6 copy-start.3
  88.4 1.4 %collective-permute-start.2 = (bf16[32,512]{1,0:T(8,128)(2,1)}, bf16[32,512]{1,0:T(8,128)(2,1)S(1)}, u32[]{:S(2)}, u32[]{:S(2)}) collective-permute-start(bf16[32,512]{1,0:T(8,128)(2,1)} %get-tuple-element.12), channel_id=1, source_target_pairs={{0,1},{1,0},{2,3},{3,2},{4,5},{5,4},{6,7},{7,6},{8,9},{9,8},{10,11... | collective-permute-start | bytes 98312 | tf_op jit(solution)/shard_map/ppermute | solution.py:183
  110.9 6.2 %copy-start.1 = (bf16[16,32,512]{2,1,0:T(8,128)(2,1)}, bf16[16,32,512]{2,1,0:T(8,128)(2,1)S(1)}, u32[]{:S(2)}) copy-start(bf16[16,32,512]{2,1,0:T(8,128)(2,1)S(1)} %all_to_all.23) | copy-start | bytes 1572868
  110.9 6.2 %collective-permute-start.3 = (bf16[512,512]{1,0:T(8,128)(2,1)S(1)}, bf16[512,512]{1,0:T(8,128)(2,1)S(1)}, u32[]{:S(2)}, u32[]{:S(2)}) collective-permute-start(bf16[512,512]{1,0:T(8,128)(2,1)S(1)} %bitcast.18), channel_id=1, source_target_pairs={{0,1},{1,0},{2,3},{3,2},{4,5},{5,4},{6,7},{7,6},{8,9},{9,8},{10,11... | collective-permute-start | bytes 1572872 | tf_op jit(solution)/shard_map/ppermute | solution.py:183
  117.1 0.8 copy-start.2

commit v2 on v1

v2 whole, which is shorter than its diff:
```python
import jax
import jax.numpy as jnp
from jax import lax
from jax.experimental import pallas as pl
from jax.experimental.pallas import tpu as pltpu
from jax.sharding import PartitionSpec as P


HEADS = 8
EXPERTS = 16
SLOTS = 64

EPS = 1e-06
LOGIT_SCALE = 3.0
MASKED = -1e30
LOG2E = 1.4426950408889634

F32 = jnp.float32
BF16 = jnp.bfloat16
VMEM = pl.BlockSpec(memory_space=pltpu.VMEM)
STAT_ROWS = 8


def nn(a, b):
    return lax.dot_general(a, b, (((1,), (0,)), ((), ())), preferred_element_type=F32)


def nt(a, b):
    return lax.dot_general(a, b, (((1,), (1,)), ((), ())), preferred_element_type=F32)


def call(kernel, out_shape, args, scratch=(), flops=1 << 20, transcendentals=0, left=0):
    single = isinstance(out_shape, jax.ShapeDtypeStruct)
    outs = (out_shape,) if single else tuple(out_shape)
    moved = sum(a.size * a.dtype.itemsize for a in (*args, *outs))
    return pl.pallas_call(
        kernel,
        out_shape=out_shape,
        in_specs=[VMEM] * (len(args) - left) + [pl.BlockSpec(memory_space=pltpu.HBM)] * left,
        out_specs=VMEM if single else tuple([VMEM] * len(outs)),
        scratch_shapes=list(scratch),
        compiler_params=pltpu.CompilerParams(vmem_limit_bytes=16 << 20),
        cost_estimate=pl.CostEstimate(
            flops=flops, bytes_accessed=moved, transcendentals=transcendentals
        ),
    )(*args)


def one_hot(rows, outer, inner):
    row = lax.broadcasted_iota(jnp.int32, (rows, rows), 0)
    col = lax.broadcasted_iota(jnp.int32, (rows, rows), 1)
    source = (row & (inner - 1)) * outer + lax.shift_right_logical(row, inner.bit_length() - 1)
    return jnp.where(col == source, 1.0, 0.0).astype(BF16)


def by_position_kernel(
    frames, positions, x_ref, gain_ref, moe_ref, o_ref, gain_out, moe_out, back_ref, x_s, sems
):
    copies = (
        pltpu.make_async_copy(x_ref, x_s, sems.at[0]),
        pltpu.make_async_copy(gain_ref, gain_out, sems.at[1]),
        pltpu.make_async_copy(moe_ref, moe_out, sems.at[2]),
    )
    for copy in copies:
        copy.start()
    order = one_hot(frames * positions, positions, frames)
    back_ref[...] = one_hot(frames * positions, frames, positions)
    for copy in copies:
        copy.wait()
    o_ref[...] = nn(order, x_s[...]).astype(BF16)


def rms(rows, gain):
    mean_sq = jnp.mean(rows * rows, axis=-1, keepdims=True)
    return (rows * lax.rsqrt(mean_sq + EPS) * gain).astype(BF16)


def attention_kernel(x_ref, gain_ref, wq_ref, wk_ref, wv_ref, o_ref, n_s, q_s, k_s, v_s):
    frames, features = x_ref.shape
    n_s[...] = rms(x_ref[...].astype(F32), gain_ref[...])
    q_s[...] = nn(n_s[...], wq_ref[...]).astype(BF16)
    k_s[...] = nn(n_s[...], wk_ref[...]).astype(BF16)
    v_s[...] = nn(n_s[...], wv_ref[...]).astype(BF16)
    head_dim = features // HEADS
    scale = head_dim ** (-0.5) * LOG2E
    block = 256
    row = lax.broadcasted_iota(jnp.int32, (block, block), 0)
    col = lax.broadcasted_iota(jnp.int32, (block, block), 1)
    causal = row >= col
    low = lax.broadcasted_iota(jnp.int32, (1, 128), 1) < head_dim
    for pair in range(features // 128):
        lanes = slice(pair * 128, pair * 128 + 128)
        for start in range(0, frames, block):
            count = start + block
            mixed = []
            for mine in (low, jnp.logical_not(low)):
                q = jnp.where(mine, q_s[start:count, lanes], jnp.zeros((), BF16))
                t = nt(q, k_s[:count, lanes]) * scale
                last = jnp.where(causal, t[:, start:], MASKED)
                t = last if start == 0 else jnp.concatenate([t[:, :start], last], axis=1)
                weights = jnp.exp2(t - jnp.max(t, axis=1, keepdims=True)).astype(BF16)
                v = jnp.where(mine, v_s[:count, lanes], jnp.ones((), BF16))
                both = nn(weights, v)
                mixed.append(both / pltpu.roll(both, head_dim, 1))
            o_ref[start:count, lanes] = jnp.where(low, mixed[0], mixed[1]).astype(BF16)


def residual_kernel(mixed_ref, x_ref, wo_ref, gain_ref, r_ref, m_ref):
    r = (x_ref[...].astype(F32) + nn(mixed_ref[...], wo_ref[...])).astype(BF16)
    r_ref[...] = r
    m_ref[...] = rms(r.astype(F32), gain_ref[...])


def keys_kernel(keys_ref, slots_ref):
    half = SLOTS // 2
    core = lax.rem(lax.axis_index("pos"), 2)
    row = lax.broadcasted_iota(jnp.int32, (128, 256), 0)
    col = lax.broadcasted_iota(jnp.int32, (128, 256), 1)
    first = (row // half) * SLOTS + (row & (half - 1))
    count = keys_ref.shape[1] // 2
    for turn in range(2):
        taken = core if turn == 0 else 1 - core
        pick = jnp.where(col == first + taken * half, 1.0, 0.0).astype(BF16)
        for k in range(count // 128):
            at = turn * count + k * 128
            keys = nt(pick, keys_ref[:, 256 * k : 256 * k + 256])
            slots_ref[at : at + 128, :] = keys.astype(BF16)


def combine_kernel(m_ref, slots_ref, c_ref):
    rows = 256
    for start in range(0, m_ref.shape[0], rows):
        part = slice(start, start + rows)
        t = nt(m_ref[part, :], slots_ref[...]) * (LOGIT_SCALE * LOG2E)
        w = jnp.exp2(t - jnp.max(t, axis=1, keepdims=True))
        c_ref[part, :] = (w / jnp.sum(w, axis=1, keepdims=True)).astype(BF16)


def dispatch_kernel(m_ref, other_ref, keys_ref, o_ref, all_s):
    tokens, features = m_ref.shape
    all_s[:tokens, :] = m_ref[...]
    all_s[tokens:, :] = other_ref[...]
    half = SLOTS // 2
    rows = 256
    for start in range(0, keys_ref.shape[0] // 2, rows):
        t = nt(keys_ref[start : start + rows, :], all_s[...]) * (LOGIT_SCALE * LOG2E)
        largest = jnp.max(t, axis=1, keepdims=True)
        w = jnp.exp2(t - largest)
        total = jnp.sum(w, axis=1, keepdims=True)
        sums = (nn(w.astype(BF16), all_s[...]) / total).astype(BF16)
        for k in range(rows // half):
            expert = start // half + k
            for j in range(features // 128):
                o_ref[expert, j * half : (j + 1) * half, :] = sums[
                    k * half : (k + 1) * half, j * 128 : (j + 1) * 128
                ]
        column = largest + jnp.log2(total)
        for at in range(0, rows, 128):
            lse = jnp.broadcast_to(column[at : at + 128], (128, 128)).T[:STAT_ROWS, :]
            high = lse.astype(BF16).astype(F32)
            middle = (lse - high).astype(BF16).astype(F32)
            rest = lse - high - middle
            line = lax.broadcasted_iota(jnp.int32, lse.shape, 0)
            stats = jnp.where(
                line == 0, high, jnp.where(line == 1, middle, jnp.where(line == 2, rest, 0.0))
            ).astype(BF16)
            for k in range(128 // half):
                o_ref[(start + at) // half + k, features // 128 * half :, :] = stats


def expert_kernel(got_ref, w_in_ref, other_in_ref, w_out_ref, other_out_ref, o_ref, w_s):
    chips, half, features = o_ref.shape
    tall = features // 128 * half
    lse = jnp.concatenate(
        [
            jnp.sum(got_ref[s, tall:, :].astype(F32), axis=0, keepdims=True)
            for s in range(chips)
        ],
        axis=0,
    )
    w = jnp.exp2(lse - jnp.max(lse, axis=0, keepdims=True))
    w = w / jnp.sum(w, axis=0, keepdims=True)
    w_s[...] = jnp.concatenate([w, jnp.zeros((128 - chips, 128), F32)], axis=0).T
    place = lax.rem(lax.axis_index("pos") // 2, 128 // half)
    mine = w_s[pl.ds(pl.multiple_of(place * half, half), half), :]
    columns = []
    for j in range(features // 128):
        total = jnp.zeros((half, 128), F32)
        for s in range(chips):
            total += mine[:, s : s + 1] * got_ref[s, j * half : (j + 1) * half, :].astype(F32)
        columns.append(total.astype(BF16))
    slot_in = jnp.concatenate(columns, axis=1)
    out = jnp.zeros((half, features), F32)
    for first, second in ((w_in_ref, w_out_ref), (other_in_ref, other_out_ref)):
        hidden = jax.nn.gelu(nn(slot_in, first[...])).astype(BF16)
        out += nn(hidden, second[...]).astype(BF16).astype(F32)
    out = out.astype(BF16)
    for s in range(chips):
        o_ref[s] = out


def own_kernel(r_ref, c_ref, own_ref, o_ref):
    count = own_ref.shape[0]
    o_ref[...] = r_ref[...].astype(F32) + nn(c_ref[:, :count], own_ref[...])


def output_kernel(sum_ref, c_ref, other_ref, back_ref, o_ref):
    count = other_ref.shape[0]
    out = (sum_ref[...] + nn(c_ref[:, count:], other_ref[...])).astype(BF16)
    o_ref[...] = nn(back_ref[...], out).astype(BF16)


def from_other_core(block):
    return lax.ppermute(block, "pos", [(k, k ^ 1) for k in range(lax.axis_size("pos"))])


def local(
    frames_in, attn_gain, w_query, w_key, w_value, w_output, moe_gain, dispatch_keys, w_in, w_out
):
    frame_count, pos_count, features = frames_in.shape
    tokens = frame_count * pos_count
    chips = lax.axis_size("pos") // 2
    half = SLOTS // 2
    by_core = [[2 * chip + core for chip in range(chips)] for core in range(2)]
    wide = jax.ShapeDtypeStruct((tokens, features), BF16)

    def by_position(*refs):
        by_position_kernel(frame_count, pos_count, *refs)

    def over_frames(block):
        block = block.reshape(pos_count, frame_count, features)
        block = lax.all_to_all(block, "frame", split_axis=0, concat_axis=0, tiled=True)
        return block.reshape(tokens, features)

    def over_chips(blocks):
        return lax.all_to_all(
            blocks, "pos", split_axis=0, concat_axis=0, tiled=True, axis_index_groups=by_core
        )

    other_in = from_other_core(w_in[0])
    other_out = from_other_core(w_out[0])
    line = jax.ShapeDtypeStruct((1, features), F32)
    x, gain, gain_moe, back = call(
        by_position,
        (wide, line, line, jax.ShapeDtypeStruct((tokens, tokens), BF16)),
        (frames_in.reshape(tokens, features), attn_gain.reshape(1, -1), moe_gain.reshape(1, -1)),
        scratch=[pltpu.VMEM((tokens, features), BF16), pltpu.SemaphoreType.DMA((3,))],
        left=3,
        flops=2 * tokens**2 * features,
    )
    mixed = call(
        attention_kernel,
        wide,
        (over_frames(x), gain, w_query, w_key, w_value),
        scratch=[pltpu.VMEM((tokens, features), BF16)] * 4,
        flops=14 * tokens**2 * features,
        transcendentals=HEADS * tokens**2,
    )
    residual, moe_input = call(
        residual_kernel,
        (wide, wide),
        (over_frames(mixed), x, w_output, gain_moe),
        flops=2 * tokens**2 * features,
    )
    other_input = from_other_core(moe_input)
    slot_keys = call(
        keys_kernel,
        jax.ShapeDtypeStruct((EXPERTS * SLOTS, features), BF16),
        (dispatch_keys,),
        flops=512 * tokens * features,
    )
    sums = call(
        dispatch_kernel,
        jax.ShapeDtypeStruct((chips, features // 128 * half + STAT_ROWS, 128), BF16),
        (moe_input, other_input, slot_keys),
        scratch=[pltpu.VMEM((2 * tokens, features), BF16)],
        flops=8 * tokens**2 * features,
        transcendentals=2 * tokens**2,
    )
    outputs = call(
        expert_kernel,
        jax.ShapeDtypeStruct((chips, half, features), BF16),
        (over_chips(sums), w_in[0], other_in, w_out[0], other_out),
        scratch=[pltpu.VMEM((128, 128), F32)],
        flops=16 * SLOTS * features**2,
    )
    own_half = over_chips(outputs).reshape(-1, features)
    other_half = from_other_core(own_half)
    combine = call(
        combine_kernel,
        jax.ShapeDtypeStruct((tokens, EXPERTS * SLOTS), BF16),
        (moe_input, slot_keys),
        flops=4 * tokens**2 * features,
        transcendentals=2 * tokens**2,
    )
    own_sum = call(
        own_kernel,
        jax.ShapeDtypeStruct((tokens, features), F32),
        (residual, combine, own_half),
        flops=2 * tokens**2 * features,
    )
    out = call(
        output_kernel, wide, (own_sum, combine, other_half, back), flops=4 * tokens**2 * features
    )
    return out.reshape(frame_count, pos_count, features)


def solution(mesh):
    in_specs = (
        P("frame", "pos", None),
        P(),
        P(),
        P(),
        P(),
        P(),
        P(),
        P(),
        P("pos", None, None),
        P("pos", None, None),
    )
    out_specs = P("frame", "pos", None)

    return jax.shard_map(local, mesh=mesh, in_specs=in_specs, out_specs=out_specs, check_vma=False)
```

time: 122 us -> 101 us (0.83)
  blocking collectives: 76.5 us -> 46.4 us
  waiting for transfers between devices: 2.48 us -> 18.3 us
  Pallas kernels: 29.6 us -> 16.4 us
  starting transfers between devices: 8.47 us -> 17.3 us
  local copies, waits for them, and re-layouts: 3.63 us -> 1.79 us
    all_to_all x4 -> x3, blocking collectives: 76.5 us -> 46.4 us  [the longest x2 24.7 us: over_frames(): lax.all_to_all(block, 'frame', split_axis=0, concat_axis=0, tiled=True)]
    all_to_all x0 -> x1, waiting for transfers between devices: none -> 18.1 us  [over_chips(): lax.all_to_all(blocks, 'pos', split_axis=0, concat_axis=0, tiled=True, ax...]
    pallas_call x8 -> x9, Pallas kernels: 29.6 us -> 16.4 us  [call(): pl.pallas_call(kernel, out_shape=out_shape, in_specs=[VMEM] * (len(args)...]
    all_to_all x0 -> x1, starting transfers between devices: none -> 10.6 us  [over_chips(): lax.all_to_all(blocks, 'pos', split_axis=0, concat_axis=0, tiled=True, ax...]
    ppermute x4, waiting for transfers between devices: 2.48 us -> 0.19 us  [from_other_core(): lax.ppermute(block, 'pos', [(k, k ^ 1) for k in range(lax.axis_size('pos'...]
    ppermute x4, starting transfers between devices: 8.47 us -> 6.62 us  [from_other_core(): lax.ppermute(block, 'pos', [(k, k ^ 1) for k in range(lax.axis_size('pos'...]
    unnamed x11 -> x26, local copies, waits for them, and re-layouts: 2.73 us -> 1.79 us
  transfers between devices with their start and end apart: 4 -> 5, of which waited for: 3 -> 2; matrix products, arithmetic and copies ran while one was open for 1% -> 0% of each run, Pallas kernels for 3% -> 5%
where the time goes in v2:
time: 101 us; the launch traced here: 100 us
  blocking collectives  46.4 us (46%)
  waiting for transfers between devices  18.3 us (18%)
  starting transfers between devices  17.3 us (17%)
  Pallas kernels  16.4 us (16%)
  local copies, waits for them, and re-layouts  1.79 us (2%)
    all_to_all x2, blocking collectives, over_frames(): lax.all_to_all(block, 'frame', split_axis=0, concat_axis=0, tiled=True)  24.7 us
    all_to_all x1, blocking collectives, over_chips(): lax.all_to_all(blocks, 'pos', split_axis=0, concat_axis=0, tiled=True, ax...  21.7 us
    all_to_all x1, waiting for transfers between devices, over_chips(): lax.all_to_all(blocks, 'pos', split_axis=0, concat_axis=0, tiled=True, ax...  18.1 us
    pallas_call x9, Pallas kernels, call(): pl.pallas_call(kernel, out_shape=out_shape, in_specs=[VMEM] * (len(args)...  16.4 us
    all_to_all x1, starting transfers between devices, over_chips(): lax.all_to_all(blocks, 'pos', split_axis=0, concat_axis=0, tiled=True, ax...  10.6 us
    ppermute x4, starting transfers between devices, from_other_core(): lax.ppermute(block, 'pos', [(k, k ^ 1) for k in range(lax.axis_size('pos'...  6.62 us
  transfers between devices with their start and end apart: 5, of which 2 were waited for; matrix products, arithmetic and copies ran while one was open for 0% of the time, Pallas kernels for 5%

profile of v2, /device:TPU:1, one launch (start us, length us, event | category | flops | bytes accessed | tf_op | source)
XLA Modules:
  0.0 100.2 jit_solution(3971434135686211184)
XLA Ops:
  0.0 0.7 copy-done.12
  0.7 0.0 copy-done.11
  0.7 1.0 %copy-done.7 = bf16[64,8,512]{2,1,0:T(8,128)(2,1)S(1)} copy-done((bf16[64,8,512]{2,1,0:T(8,128)(2,1)S(1)}, bf16[64,8,512]{2,1,0:T(8,128)(2,1)}, u32[]{:S(2)}) %copy-start.7) | copy-done | bytes 524312
  1.7 0.8 shard_map.100
  2.5 0.0 copy-start.8
  2.6 0.0 copy-start.9
  2.6 14.4 %all_to_all.20 = bf16[8,64,512]{2,1,0:T(8,128)(2,1)S(1)} all-to-all(bf16[8,64,512]{2,1,0:T(8,128)(2,1)S(1)} %bitcast.11), channel_id=1, replica_groups=mesh['frame'=8,'pos'=32] {'frame'}, dimensions={0} | all-to-all | bytes 1048576 | tf_op jit(solution)/shard_map/all_to_all | solution.py:232
  17.0 0.0 copy-done.10
  17.0 0.0 copy-start.4
  17.0 5.4 %shard_map.101 = bf16[512,512]{1,0:T(8,128)(2,1)S(1)} custom-call(bf16[512,512]{1,0:T(8,128)(2,1)S(1)} %bitcast.18, f32[1,512]{1,0:T(1,128)S(1)} %get-tuple-element.12.gain_ref, bf16[512,512]{1,0:T(8,128)(2,1)S(1)} %copy-done.8, bf16[512,512]{1,0:T(8,128)(2,1)S(1)} %copy-done.9, bf16[512,512]{1,0:T(8,128)(2,1)S(1)} %copy-done.10), custom_call_target="tpu_custom_call" | custom-call | flops 1879048192 | bytes 2623488 | tf_op jit(solution)/shard_map/pallas_call | solution.py:36
  22.4 0.0 copy-start.1
  22.4 10.3 %all_to_all.21 = bf16[8,64,512]{2,1,0:T(8,128)(2,1)S(1)} all-to-all(bf16[8,64,512]{2,1,0:T(8,128)(2,1)S(1)} %bitcast.17), channel_id=1, replica_groups=mesh['frame'=8,'pos'=32] {'frame'}, dimensions={0} | all-to-all | bytes 1048576 | tf_op jit(solution)/shard_map/all_to_all | solution.py:232
  32.7 0.7 shard_map.102
  33.4 0.0 copy-start.5
  33.4 0.0 copy-start.2
  33.4 3.5 %collective-permute-start = (bf16[512,512]{1,0:T(8,128)(2,1)S(1)}, bf16[512,512]{1,0:T(8,128)(2,1)S(1)}, u32[]{:S(2)}, u32[]{:S(2)}) collective-permute-start(bf16[512,512]{1,0:T(8,128)(2,1)S(1)} %get-tuple-element.15.m_ref), channel_id=1, source_target_pairs={{0,1},{1,0},{2,3},{3,2},{4,5},{5,4},{6,7},{7,6},{8,9},{9,8},{10,11... | collective-permute-start | bytes 1572872 | tf_op jit(solution)/shard_map/ppermute | solution.py:214
  36.9 0.4 collective-permute-start.1
  37.4 0.1 collective-permute-start.2
  37.5 0.8 shard_map.103.slots_ref.keys_ref
  38.3 0.2 collective-permute-done.other_ref
  38.5 2.6 %shard_map.105 = bf16[16,136,128]{2,1,0:T(8,128)(2,1)} custom-call(bf16[512,512]{1,0:T(8,128)(2,1)S(1)} %get-tuple-element.15.m_ref, bf16[512,512]{1,0:T(8,128)(2,1)S(1)} %collective-permute-done.other_ref, bf16[1024,512]{1,0:T(8,128)(2,1)S(1)} %shard_map.103.slots_ref.keys_ref), custom_call_target="tpu_custom_call" | custom-call | flops 1073741824 | bytes 2654208 | tf_op jit(solution)/shard_map/pallas_call | solution.py:36
  41.0 10.6 %all-to-all-start.2 = ((bf16[16,136,128]{2,1,0:T(8,128)(2,1)}), bf16[16,136,128]{2,1,0:T(8,128)(2,1)S(1)}, u32[]{:S(2)}, u32[]{:S(2)}) async-start(bf16[16,136,128]{2,1,0:T(8,128)(2,1)} %shard_map.105), calls=%async_computation.2 | async-start | bytes 1114112 | tf_op jit(solution)/shard_map/all_to_all | solution.py:236
  51.7 0.0 collective-permute-done.1.other_in_ref
  51.7 0.0 collective-permute-done.2.other_out_ref
  51.7 18.1 %all-to-all-done.2.got_ref = bf16[16,136,128]{2,1,0:T(8,128)(2,1)S(1)} async-done(((bf16[16,136,128]{2,1,0:T(8,128)(2,1)}), bf16[16,136,128]{2,1,0:T(8,128)(2,1)S(1)}, u32[]{:S(2)}, u32[]{:S(2)}) %all-to-all-start.2) | async-done | bytes 557088 | tf_op jit(solution)/shard_map/all_to_all | solution.py:236
  69.8 3.0 %shard_map.106 = bf16[16,32,512]{2,1,0:T(8,128)(2,1)S(1)} custom-call(bf16[16,136,128]{2,1,0:T(8,128)(2,1)S(1)} %all-to-all-done.2.got_ref, bf16[512,1024]{1,0:T(8,128)(2,1)S(1)} %bitcast.16, bf16[512,1024]{1,0:T(8,128)(2,1)} %collective-permute-done.1.other_in_ref, bf16[1024,512]{1,0:T(8,128)(2,1)} %bitcast.8.w_out_ref, ...), custom_call_target="tpu_custom_call" | custom-call | flops 268435456 | bytes 5275648 | tf_op jit(solution)/shard_map/pallas_call | solution.py:36
  72.8 21.7 %all_to_all.22 = bf16[16,32,512]{2,1,0:T(8,128)(2,1)S(1)} all-to-all(bf16[16,32,512]{2,1,0:T(8,128)(2,1)S(1)} %shard_map.106), channel_id=1, replica_groups={{0,2,4,6,8,10,12,14,16,18,20,22,24,26,28,30},{1,3,5,7,9,11,13,15,17,19,..., dimensions={0} | all-to-all | bytes 1048576 | tf_op jit(solution)/shard_map/all_to_all | solution.py:236
  94.5 2.6 %collective-permute-start.3 = (bf16[512,512]{1,0:T(8,128)(2,1)S(1)}, bf16[512,512]{1,0:T(8,128)(2,1)S(1)}, u32[]{:S(2)}, u32[]{:S(2)}) collective-permute-start(bf16[512,512]{1,0:T(8,128)(2,1)S(1)} %bitcast.13), channel_id=1, source_target_pairs={{0,1},{1,0},{2,3},{3,2},{4,5},{5,4},{6,7},{7,6},{8,9},{9,8},{10,11... | collective-permute-start | bytes 1572872 | tf_op jit(solution)/shard_map/ppermute | solution.py:214
  97.1 1.1 %shard_map.104.c_ref = bf16[512,1024]{1,0:T(8,128)(2,1)S(1)} custom-call(bf16[512,512]{1,0:T(8,128)(2,1)S(1)} %copy-done.3, bf16[1024,512]{1,0:T(8,128)(2,1)S(1)} %shard_map.103.slots_ref.keys_ref), custom_call_target="tpu_custom_call" | custom-call | flops 536870912 | bytes 2621440 | tf_op jit(solution)/shard_map/pallas_call | solution.py:36
  98.2 0.4 shard_map.107.sum_ref
  98.6 0.0 collective-permute-done.3.other_ref
  98.7 1.6 %shard_map.108 = bf16[512,512]{1,0:T(8,128)(2,1)} custom-call(f32[512,512]{1,0:T(8,128)S(1)} %shard_map.107.sum_ref, bf16[512,1024]{1,0:T(8,128)(2,1)S(1)} %shard_map.104.c_ref, bf16[512,512]{1,0:T(8,128)(2,1)S(1)} %collective-permute-done.3.other_ref, bf16[512,512]{1,0:T(8,128)(2,1)S(1)} %get-tuple-element.16.back_ref), custom_call_target="tpu_custom_call" | custom-call | flops 536870912 | bytes 3670016 | tf_op jit(solution)/shard_map/pallas_call | solution.py:36
  (16 shorter events, 0.0 us)
Async XLA Ops:
  0.0 0.7 copy-start.12
  0.0 0.7 copy-start.11
  0.7 1.0 %copy-start.7 = (bf16[64,8,512]{2,1,0:T(8,128)(2,1)S(1)}, bf16[64,8,512]{2,1,0:T(8,128)(2,1)}, u32[]{:S(2)}) copy-start(bf16[64,8,512]{2,1,0:T(8,128)(2,1)} %param.10) | copy-start | bytes 1572868
  1.7 15.3 %copy-start.10 = (bf16[512,512]{1,0:T(8,128)(2,1)S(1)}, bf16[512,512]{1,0:T(8,128)(2,1)}, u32[]{:S(2)}) copy-start(bf16[512,512]{1,0:T(8,128)(2,1)} %wv_ref.1) | copy-start | bytes 1572868
  2.5 14.5 %copy-start.8 = (bf16[512,512]{1,0:T(8,128)(2,1)S(1)}, bf16[512,512]{1,0:T(8,128)(2,1)}, u32[]{:S(2)}) copy-start(bf16[512,512]{1,0:T(8,128)(2,1)} %wq_ref.1) | copy-start | bytes 1572868
  2.6 14.5 %copy-start.9 = (bf16[512,512]{1,0:T(8,128)(2,1)S(1)}, bf16[512,512]{1,0:T(8,128)(2,1)}, u32[]{:S(2)}) copy-start(bf16[512,512]{1,0:T(8,128)(2,1)} %wk_ref.1) | copy-start | bytes 1572868
  17.0 15.7 %copy-start.4 = (bf16[512,512]{1,0:T(8,128)(2,1)S(1)}, bf16[512,512]{1,0:T(8,128)(2,1)}, u32[]{:S(2)}) copy-start(bf16[512,512]{1,0:T(8,128)(2,1)} %wo_ref.1) | copy-start | bytes 1572868
  22.4 15.0 %copy-start.1 = (bf16[512,1024]{1,0:T(8,128)(2,1)S(1)}, bf16[512,1024]{1,0:T(8,128)(2,1)}, u32[]{:S(2)}) copy-start(bf16[512,1024]{1,0:T(8,128)(2,1)} %keys_ref.1) | copy-start | bytes 3145732
  32.7 4.2 %copy-start = (bf16[1,512,1024]{2,1,0:T(8,128)(2,1)S(1)}, bf16[1,512,1024]{2,1,0:T(8,128)(2,1)}, u32[]{:S(2)}) copy-start(bf16[1,512,1024]{2,1,0:T(8,128)(2,1)} %param.18) | copy-start | bytes 3145732
  33.4 4.9 %copy-start.5 = (bf16[512,512]{1,0:T(8,128)(2,1)}, bf16[512,512]{1,0:T(8,128)(2,1)S(1)}, u32[]{:S(2)}) copy-start(bf16[512,512]{1,0:T(8,128)(2,1)S(1)} %get-tuple-element.14.r_ref) | copy-start | bytes 1572868
  33.4 5.1 %copy-start.2 = (bf16[512,512]{1,0:T(8,128)(2,1)}, bf16[512,512]{1,0:T(8,128)(2,1)S(1)}, u32[]{:S(2)}) copy-start(bf16[512,512]{1,0:T(8,128)(2,1)S(1)} %get-tuple-element.15.m_ref) | copy-start | bytes 1572868
  33.4 5.0 %collective-permute-start = (bf16[512,512]{1,0:T(8,128)(2,1)S(1)}, bf16[512,512]{1,0:T(8,128)(2,1)S(1)}, u32[]{:S(2)}, u32[]{:S(2)}) collective-permute-start(bf16[512,512]{1,0:T(8,128)(2,1)S(1)} %get-tuple-element.15.m_ref), channel_id=1, source_target_pairs={{0,1},{1,0},{2,3},{3,2},{4,5},{5,4},{6,7},{7,6},{8,9},{9,8},{10,11... | collective-permute-start | bytes 1572872 | tf_op jit(solution)/shard_map/ppermute | solution.py:214
  36.9 14.7 %collective-permute-start.1 = (bf16[512,1024]{1,0:T(8,128)(2,1)S(1)}, bf16[512,1024]{1,0:T(8,128)(2,1)}, u32[]{:S(2)}, u32[]{:S(2)}) collective-permute-start(bf16[512,1024]{1,0:T(8,128)(2,1)S(1)} %bitcast.15), channel_id=1, source_target_pairs={{0,1},{1,0},{2,3},{3,2},{4,5},{5,4},{6,7},{7,6},{8,9},{9,8},{10,11... | collective-permute-start | bytes 3145736 | tf_op jit(solution)/shard_map/ppermute | solution.py:214
  37.4 14.3 %collective-permute-start.2 = (bf16[1024,512]{1,0:T(8,128)(2,1)}, bf16[1024,512]{1,0:T(8,128)(2,1)}, u32[]{:S(2)}, u32[]{:S(2)}) collective-permute-start(bf16[1024,512]{1,0:T(8,128)(2,1)} %bitcast.8.w_out_ref), channel_id=1, source_target_pairs={{0,1},{1,0},{2,3},{3,2},{4,5},{5,4},{6,7},{7,6},{8,9},{9,8},{10,11... | collective-permute-start | bytes 3145736 | tf_op jit(solution)/shard_map/ppermute | solution.py:214
  41.0 28.8 %all-to-all-start.2 = ((bf16[16,136,128]{2,1,0:T(8,128)(2,1)}), bf16[16,136,128]{2,1,0:T(8,128)(2,1)S(1)}, u32[]{:S(2)}, u32[]{:S(2)}) async-start(bf16[16,136,128]{2,1,0:T(8,128)(2,1)} %shard_map.105), calls=%async_computation.2 | async-start | bytes 1114112 | tf_op jit(solution)/shard_map/all_to_all | solution.py:236
  72.8 24.3 %copy-start.3 = (bf16[512,512]{1,0:T(8,128)(2,1)S(1)}, bf16[512,512]{1,0:T(8,128)(2,1)}, u32[]{:S(2)}) copy-start(bf16[512,512]{1,0:T(8,128)(2,1)} %copy-done.2) | copy-start | bytes 1572868
  94.5 3.7 %copy-start.6 = (bf16[512,512]{1,0:T(8,128)(2,1)S(1)}, bf16[512,512]{1,0:T(8,128)(2,1)}, u32[]{:S(2)}) copy-start(bf16[512,512]{1,0:T(8,128)(2,1)} %copy-done.5) | copy-start | bytes 1572868
  94.5 4.1 %collective-permute-start.3 = (bf16[512,512]{1,0:T(8,128)(2,1)S(1)}, bf16[512,512]{1,0:T(8,128)(2,1)S(1)}, u32[]{:S(2)}, u32[]{:S(2)}) collective-permute-start(bf16[512,512]{1,0:T(8,128)(2,1)S(1)} %bitcast.13), channel_id=1, source_target_pairs={{0,1},{1,0},{2,3},{3,2},{4,5},{5,4},{6,7},{7,6},{8,9},{9,8},{10,11... | collective-permute-start | bytes 1572872 | tf_op jit(solution)/shard_map/ppermute | solution.py:214

commit v3 on v2

--- a/solution.py
+++ b/solution.py
@@ -19,6 +19,7 @@
 BF16 = jnp.bfloat16
 VMEM = pl.BlockSpec(memory_space=pltpu.VMEM)
 STAT_ROWS = 8
+ORDER = tuple(2 * z + y for y in range(2) for z in range(8))
 
 
 def nn(a, b):
@@ -75,34 +76,39 @@
     return (rows * lax.rsqrt(mean_sq + EPS) * gain).astype(BF16)
 
 
-def attention_kernel(x_ref, gain_ref, wq_ref, wk_ref, wv_ref, o_ref, n_s, q_s, k_s, v_s):
+def attention_kernel(x_ref, gain_ref, wq_ref, wk_ref, wv_ref, o_ref, n_s, q_s, k_s, v_s, w_s):
     frames, features = x_ref.shape
+    head_dim = features // HEADS
     n_s[...] = rms(x_ref[...].astype(F32), gain_ref[...])
-    q_s[...] = nn(n_s[...], wq_ref[...]).astype(BF16)
+    q_s[...] = (nn(n_s[...], wq_ref[...]) * (head_dim ** (-0.5) * LOG2E)).astype(BF16)
     k_s[...] = nn(n_s[...], wk_ref[...]).astype(BF16)
     v_s[...] = nn(n_s[...], wv_ref[...]).astype(BF16)
-    head_dim = features // HEADS
-    scale = head_dim ** (-0.5) * LOG2E
-    block = 256
-    row = lax.broadcasted_iota(jnp.int32, (block, block), 0)
-    col = lax.broadcasted_iota(jnp.int32, (block, block), 1)
+    half = frames // 2
+    row = lax.broadcasted_iota(jnp.int32, (half, half), 0)
+    col = lax.broadcasted_iota(jnp.int32, (half, half), 1)
     causal = row >= col
     low = lax.broadcasted_iota(jnp.int32, (1, 128), 1) < head_dim
+    w_s[:half, half:] = jnp.zeros((half, half), BF16)
     for pair in range(features // 128):
         lanes = slice(pair * 128, pair * 128 + 128)
-        for start in range(0, frames, block):
-            count = start + block
-            mixed = []
-            for mine in (low, jnp.logical_not(low)):
-                q = jnp.where(mine, q_s[start:count, lanes], jnp.zeros((), BF16))
-                t = nt(q, k_s[:count, lanes]) * scale
-                last = jnp.where(causal, t[:, start:], MASKED)
-                t = last if start == 0 else jnp.concatenate([t[:, :start], last], axis=1)
-                weights = jnp.exp2(t - jnp.max(t, axis=1, keepdims=True)).astype(BF16)
-                v = jnp.where(mine, v_s[:count, lanes], jnp.ones((), BF16))
-                both = nn(weights, v)
-                mixed.append(both / pltpu.roll(both, head_dim, 1))
-            o_ref[start:count, lanes] = jnp.where(low, mixed[0], mixed[1]).astype(BF16)
+        mixed = []
+        for mine in (low, jnp.logical_not(low)):
+            q = jnp.where(mine, q_s[:, lanes], jnp.zeros((), BF16))
+            t = nt(q, k_s[:, lanes])
+            first = jnp.where(causal, t[:half, :half], MASKED)
+            w = jnp.exp2(first - jnp.max(first, axis=1, keepdims=True))
+            w_s[:half, :half] = w.astype(BF16)
+            before = t[half:, :half]
+            last = jnp.where(causal, t[half:, half:], MASKED)
+            largest = jnp.maximum(
+                jnp.max(before, axis=1, keepdims=True), jnp.max(last, axis=1, keepdims=True)
+            )
+            w_s[half:, :half] = jnp.exp2(before - largest).astype(BF16)
+            w_s[half:, half:] = jnp.exp2(last - largest).astype(BF16)
+            v = jnp.where(mine, v_s[:, lanes], jnp.ones((), BF16))
+            mixed.append(nn(w_s[...], v))
+        total = pltpu.roll(jnp.where(low, mixed[1], mixed[0]), head_dim, 1)
+        o_ref[:, lanes] = (jnp.where(low, mixed[0], mixed[1]) / total).astype(BF16)
 
 
 def residual_kernel(mixed_ref, x_ref, wo_ref, gain_ref, r_ref, m_ref):
@@ -122,9 +128,10 @@
         taken = core if turn == 0 else 1 - core
         pick = jnp.where(col == first + taken * half, 1.0, 0.0).astype(BF16)
         for k in range(count // 128):
-            at = turn * count + k * 128
-            keys = nt(pick, keys_ref[:, 256 * k : 256 * k + 256])
-            slots_ref[at : at + 128, :] = keys.astype(BF16)
+            keys = nt(pick, keys_ref[:, 256 * k : 256 * k + 256]).astype(BF16)
+            for i in range(128 // half):
+                at = turn * count + half * ORDER.index(k * (128 // half) + i)
+                slots_ref[at : at + half, :] = keys[i * half : (i + 1) * half, :]
 
 
 def combine_kernel(m_ref, slots_ref, c_ref):
@@ -181,7 +188,9 @@
     w = jnp.exp2(lse - jnp.max(lse, axis=0, keepdims=True))
     w = w / jnp.sum(w, axis=0, keepdims=True)
     w_s[...] = jnp.concatenate([w, jnp.zeros((128 - chips, 128), F32)], axis=0).T
-    place = lax.rem(lax.axis_index("pos") // 2, 128 // half)
+    chip = lax.axis_index("pos") // 2
+    place = sum(jnp.where(chip == ORDER[k], k, 0) for k in range(chips))
+    place = lax.rem(place, 128 // half)
     mine = w_s[pl.ds(pl.multiple_of(place * half, half), half), :]
     columns = []
     for j in range(features // 128):
@@ -221,7 +230,7 @@
     tokens = frame_count * pos_count
     chips = lax.axis_size("pos") // 2
     half = SLOTS // 2
-    by_core = [[2 * chip + core for chip in range(chips)] for core in range(2)]
+    by_core = [[2 * chip + core for chip in ORDER] for core in range(2)]
     wide = jax.ShapeDtypeStruct((tokens, features), BF16)
 
     def by_position(*refs):
@@ -252,7 +261,7 @@
         attention_kernel,
         wide,
         (over_frames(x), gain, w_query, w_key, w_value),
-        scratch=[pltpu.VMEM((tokens, features), BF16)] * 4,
+        scratch=[pltpu.VMEM((tokens, features), BF16)] * 4 + [pltpu.VMEM((tokens, tokens), BF16)],
         flops=14 * tokens**2 * features,
         transcendentals=HEADS * tokens**2,
     )

time: 101 us -> 97.2 us (0.962)
  waiting for transfers between devices: 18.3 us -> 16 us
  Pallas kernels: 16.4 us -> 14.7 us
    all_to_all x1, waiting for transfers between devices: 18.1 us -> 15.8 us  [over_chips(): lax.all_to_all(blocks, 'pos', split_axis=0, concat_axis=0, tiled=True, ax...]
    pallas_call x9, Pallas kernels: 16.4 us -> 14.7 us  [call(): pl.pallas_call(kernel, out_shape=out_shape, in_specs=[VMEM] * (len(args)...]
where the time goes in v3:
time: 97.2 us; the launch traced here: 96.7 us
  blocking collectives  46.9 us (48%)
  starting transfers between devices  17.2 us (18%)
  waiting for transfers between devices  16 us (16%)
  Pallas kernels  14.7 us (15%)
  local copies, waits for them, and re-layouts  1.79 us (2%)
    all_to_all x2, blocking collectives, over_frames(): lax.all_to_all(block, 'frame', split_axis=0, concat_axis=0, tiled=True)  24.7 us
    all_to_all x1, blocking collectives, over_chips(): lax.all_to_all(blocks, 'pos', split_axis=0, concat_axis=0, tiled=True, ax...  22.1 us
    all_to_all x1, waiting for transfers between devices, over_chips(): lax.all_to_all(blocks, 'pos', split_axis=0, concat_axis=0, tiled=True, ax...  15.8 us
    pallas_call x9, Pallas kernels, call(): pl.pallas_call(kernel, out_shape=out_shape, in_specs=[VMEM] * (len(args)...  14.7 us
    all_to_all x1, starting transfers between devices, over_chips(): lax.all_to_all(blocks, 'pos', split_axis=0, concat_axis=0, tiled=True, ax...  10.6 us
    ppermute x4, starting transfers between devices, from_other_core(): lax.ppermute(block, 'pos', [(k, k ^ 1) for k in range(lax.axis_size('pos'...  6.6 us
  transfers between devices with their start and end apart: 5, of which 2 were waited for; matrix products, arithmetic and copies ran while one was open for 0% of the time, Pallas kernels for 5%

profile of v3, /device:TPU:1, one launch (start us, length us, event | category | flops | bytes accessed | tf_op | source)
XLA Modules:
  0.0 96.7 jit_solution(4998626044752331569)
XLA Ops:
  0.0 0.7 copy-done.12
  0.7 0.0 copy-done.11
  0.7 1.0 %copy-done.7 = bf16[64,8,512]{2,1,0:T(8,128)(2,1)S(1)} copy-done((bf16[64,8,512]{2,1,0:T(8,128)(2,1)S(1)}, bf16[64,8,512]{2,1,0:T(8,128)(2,1)}, u32[]{:S(2)}) %copy-start.7) | copy-done | bytes 524312
  1.7 0.8 shard_map.100
  2.5 0.0 copy-start.8
  2.6 0.0 copy-start.9
  2.6 14.4 %all_to_all.20 = bf16[8,64,512]{2,1,0:T(8,128)(2,1)S(1)} all-to-all(bf16[8,64,512]{2,1,0:T(8,128)(2,1)S(1)} %bitcast.11), channel_id=1, replica_groups=mesh['frame'=8,'pos'=32] {'frame'}, dimensions={0} | all-to-all | bytes 1048576 | tf_op jit(solution)/shard_map/all_to_all | solution.py:241
  17.0 0.0 copy-done.10
  17.0 0.0 copy-start.4
  17.0 3.7 %shard_map.101 = bf16[512,512]{1,0:T(8,128)(2,1)S(1)} custom-call(bf16[512,512]{1,0:T(8,128)(2,1)S(1)} %bitcast.18, f32[1,512]{1,0:T(1,128)S(1)} %get-tuple-element.12.gain_ref, bf16[512,512]{1,0:T(8,128)(2,1)S(1)} %copy-done.8, bf16[512,512]{1,0:T(8,128)(2,1)S(1)} %copy-done.9, bf16[512,512]{1,0:T(8,128)(2,1)S(1)} %copy-done.10), custom_call_target="tpu_custom_call" | custom-call | flops 1879048192 | bytes 2623488 | tf_op jit(solution)/shard_map/pallas_call | solution.py:37
  20.8 0.0 copy-start.1
  20.8 10.3 %all_to_all.21 = bf16[8,64,512]{2,1,0:T(8,128)(2,1)S(1)} all-to-all(bf16[8,64,512]{2,1,0:T(8,128)(2,1)S(1)} %bitcast.17), channel_id=1, replica_groups=mesh['frame'=8,'pos'=32] {'frame'}, dimensions={0} | all-to-all | bytes 1048576 | tf_op jit(solution)/shard_map/all_to_all | solution.py:241
  31.1 0.7 shard_map.102
  31.8 0.0 copy-start.5
  31.8 3.5 %collective-permute-start = (bf16[512,512]{1,0:T(8,128)(2,1)S(1)}, bf16[512,512]{1,0:T(8,128)(2,1)S(1)}, u32[]{:S(2)}, u32[]{:S(2)}) collective-permute-start(bf16[512,512]{1,0:T(8,128)(2,1)S(1)} %get-tuple-element.15.m_ref), channel_id=1, source_target_pairs={{0,1},{1,0},{2,3},{3,2},{4,5},{5,4},{6,7},{7,6},{8,9},{9,8},{10,11... | collective-permute-start | bytes 1572872 | tf_op jit(solution)/shard_map/ppermute | solution.py:223
  35.3 0.0 copy-done
  35.3 0.4 collective-permute-start.1
  35.8 0.1 collective-permute-start.2
  35.8 0.8 shard_map.103.slots_ref.keys_ref
  36.7 0.2 collective-permute-done.other_ref
  36.9 2.6 %shard_map.105 = bf16[16,136,128]{2,1,0:T(8,128)(2,1)} custom-call(bf16[512,512]{1,0:T(8,128)(2,1)S(1)} %get-tuple-element.15.m_ref, bf16[512,512]{1,0:T(8,128)(2,1)S(1)} %collective-permute-done.other_ref, bf16[1024,512]{1,0:T(8,128)(2,1)S(1)} %shard_map.103.slots_ref.keys_ref), custom_call_target="tpu_custom_call" | custom-call | flops 1073741824 | bytes 2654208 | tf_op jit(solution)/shard_map/pallas_call | solution.py:37
  39.4 10.6 %all-to-all-start.2 = ((bf16[16,136,128]{2,1,0:T(8,128)(2,1)}), bf16[16,136,128]{2,1,0:T(8,128)(2,1)S(1)}, u32[]{:S(2)}, u32[]{:S(2)}) async-start(bf16[16,136,128]{2,1,0:T(8,128)(2,1)} %shard_map.105), calls=%async_computation.2 | async-start | bytes 1114112 | tf_op jit(solution)/shard_map/all_to_all | solution.py:245
  50.0 0.0 collective-permute-done.1.other_in_ref
  50.1 0.0 collective-permute-done.2.other_out_ref
  50.1 15.8 %all-to-all-done.2.got_ref = bf16[16,136,128]{2,1,0:T(8,128)(2,1)S(1)} async-done(((bf16[16,136,128]{2,1,0:T(8,128)(2,1)}), bf16[16,136,128]{2,1,0:T(8,128)(2,1)S(1)}, u32[]{:S(2)}, u32[]{:S(2)}) %all-to-all-start.2) | async-done | bytes 557088 | tf_op jit(solution)/shard_map/all_to_all | solution.py:245
  65.8 3.0 %shard_map.106 = bf16[16,32,512]{2,1,0:T(8,128)(2,1)S(1)} custom-call(bf16[16,136,128]{2,1,0:T(8,128)(2,1)S(1)} %all-to-all-done.2.got_ref, bf16[512,1024]{1,0:T(8,128)(2,1)S(1)} %bitcast.16, bf16[512,1024]{1,0:T(8,128)(2,1)} %collective-permute-done.1.other_in_ref, bf16[1024,512]{1,0:T(8,128)(2,1)} %bitcast.8.w_out_ref, ...), custom_call_target="tpu_custom_call" | custom-call | flops 268435456 | bytes 5275648 | tf_op jit(solution)/shard_map/pallas_call | solution.py:37
  68.9 22.1 %all_to_all.22 = bf16[16,32,512]{2,1,0:T(8,128)(2,1)S(1)} all-to-all(bf16[16,32,512]{2,1,0:T(8,128)(2,1)S(1)} %shard_map.106), channel_id=1, replica_groups={{0,4,8,12,16,20,24,28,2,6,10,14,18,22,26,30},{1,5,9,13,17,21,25,29,3,7,..., dimensions={0} | all-to-all | bytes 1048576 | tf_op jit(solution)/shard_map/all_to_all | solution.py:245
  91.0 2.6 %collective-permute-start.3 = (bf16[512,512]{1,0:T(8,128)(2,1)S(1)}, bf16[512,512]{1,0:T(8,128)(2,1)S(1)}, u32[]{:S(2)}, u32[]{:S(2)}) collective-permute-start(bf16[512,512]{1,0:T(8,128)(2,1)S(1)} %bitcast.13), channel_id=1, source_target_pairs={{0,1},{1,0},{2,3},{3,2},{4,5},{5,4},{6,7},{7,6},{8,9},{9,8},{10,11... | collective-permute-start | bytes 1572872 | tf_op jit(solution)/shard_map/ppermute | solution.py:223
  93.6 1.1 %shard_map.104.c_ref = bf16[512,1024]{1,0:T(8,128)(2,1)S(1)} custom-call(bf16[512,512]{1,0:T(8,128)(2,1)S(1)} %copy-done.3, bf16[1024,512]{1,0:T(8,128)(2,1)S(1)} %shard_map.103.slots_ref.keys_ref), custom_call_target="tpu_custom_call" | custom-call | flops 536870912 | bytes 2621440 | tf_op jit(solution)/shard_map/pallas_call | solution.py:37
  94.7 0.4 shard_map.107.sum_ref
  95.1 0.0 collective-permute-done.3.other_ref
  95.1 1.6 %shard_map.108 = bf16[512,512]{1,0:T(8,128)(2,1)} custom-call(f32[512,512]{1,0:T(8,128)S(1)} %shard_map.107.sum_ref, bf16[512,1024]{1,0:T(8,128)(2,1)S(1)} %shard_map.104.c_ref, bf16[512,512]{1,0:T(8,128)(2,1)S(1)} %collective-permute-done.3.other_ref, bf16[512,512]{1,0:T(8,128)(2,1)S(1)} %get-tuple-element.16.back_ref), custom_call_target="tpu_custom_call" | custom-call | flops 536870912 | bytes 3670016 | tf_op jit(solution)/shard_map/pallas_call | solution.py:37
  (16 shorter events, 0.0 us)
Async XLA Ops:
  0.0 0.7 copy-start.12
  0.0 0.7 copy-start.11
  0.7 1.0 %copy-start.7 = (bf16[64,8,512]{2,1,0:T(8,128)(2,1)S(1)}, bf16[64,8,512]{2,1,0:T(8,128)(2,1)}, u32[]{:S(2)}) copy-start(bf16[64,8,512]{2,1,0:T(8,128)(2,1)} %param.10) | copy-start | bytes 1572868
  1.7 15.3 %copy-start.10 = (bf16[512,512]{1,0:T(8,128)(2,1)S(1)}, bf16[512,512]{1,0:T(8,128)(2,1)}, u32[]{:S(2)}) copy-start(bf16[512,512]{1,0:T(8,128)(2,1)} %wv_ref.1) | copy-start | bytes 1572868
  2.5 14.5 %copy-start.8 = (bf16[512,512]{1,0:T(8,128)(2,1)S(1)}, bf16[512,512]{1,0:T(8,128)(2,1)}, u32[]{:S(2)}) copy-start(bf16[512,512]{1,0:T(8,128)(2,1)} %wq_ref.1) | copy-start | bytes 1572868
  2.6 14.5 %copy-start.9 = (bf16[512,512]{1,0:T(8,128)(2,1)S(1)}, bf16[512,512]{1,0:T(8,128)(2,1)}, u32[]{:S(2)}) copy-start(bf16[512,512]{1,0:T(8,128)(2,1)} %wk_ref.1) | copy-start | bytes 1572868
  17.0 14.1 %copy-start.4 = (bf16[512,512]{1,0:T(8,128)(2,1)S(1)}, bf16[512,512]{1,0:T(8,128)(2,1)}, u32[]{:S(2)}) copy-start(bf16[512,512]{1,0:T(8,128)(2,1)} %wo_ref.1) | copy-start | bytes 1572868
  20.8 15.0 %copy-start.1 = (bf16[512,1024]{1,0:T(8,128)(2,1)S(1)}, bf16[512,1024]{1,0:T(8,128)(2,1)}, u32[]{:S(2)}) copy-start(bf16[512,1024]{1,0:T(8,128)(2,1)} %keys_ref.1) | copy-start | bytes 3145732
  31.1 4.2 %copy-start = (bf16[1,512,1024]{2,1,0:T(8,128)(2,1)S(1)}, bf16[1,512,1024]{2,1,0:T(8,128)(2,1)}, u32[]{:S(2)}) copy-start(bf16[1,512,1024]{2,1,0:T(8,128)(2,1)} %param.18) | copy-start | bytes 3145732
  31.8 4.9 %copy-start.5 = (bf16[512,512]{1,0:T(8,128)(2,1)}, bf16[512,512]{1,0:T(8,128)(2,1)S(1)}, u32[]{:S(2)}) copy-start(bf16[512,512]{1,0:T(8,128)(2,1)S(1)} %get-tuple-element.14.r_ref) | copy-start | bytes 1572868
  31.8 5.1 %copy-start.2 = (bf16[512,512]{1,0:T(8,128)(2,1)}, bf16[512,512]{1,0:T(8,128)(2,1)S(1)}, u32[]{:S(2)}) copy-start(bf16[512,512]{1,0:T(8,128)(2,1)S(1)} %get-tuple-element.15.m_ref) | copy-start | bytes 1572868
  31.8 5.1 %collective-permute-start = (bf16[512,512]{1,0:T(8,128)(2,1)S(1)}, bf16[512,512]{1,0:T(8,128)(2,1)S(1)}, u32[]{:S(2)}, u32[]{:S(2)}) collective-permute-start(bf16[512,512]{1,0:T(8,128)(2,1)S(1)} %get-tuple-element.15.m_ref), channel_id=1, source_target_pairs={{0,1},{1,0},{2,3},{3,2},{4,5},{5,4},{6,7},{7,6},{8,9},{9,8},{10,11... | collective-permute-start | bytes 1572872 | tf_op jit(solution)/shard_map/ppermute | solution.py:223
  35.3 14.7 %collective-permute-start.1 = (bf16[512,1024]{1,0:T(8,128)(2,1)S(1)}, bf16[512,1024]{1,0:T(8,128)(2,1)}, u32[]{:S(2)}, u32[]{:S(2)}) collective-permute-start(bf16[512,1024]{1,0:T(8,128)(2,1)S(1)} %bitcast.15), channel_id=1, source_target_pairs={{0,1},{1,0},{2,3},{3,2},{4,5},{5,4},{6,7},{7,6},{8,9},{9,8},{10,11... | collective-permute-start | bytes 3145736 | tf_op jit(solution)/shard_map/ppermute | solution.py:223
  35.8 14.3 %collective-permute-start.2 = (bf16[1024,512]{1,0:T(8,128)(2,1)}, bf16[1024,512]{1,0:T(8,128)(2,1)}, u32[]{:S(2)}, u32[]{:S(2)}) collective-permute-start(bf16[1024,512]{1,0:T(8,128)(2,1)} %bitcast.8.w_out_ref), channel_id=1, source_target_pairs={{0,1},{1,0},{2,3},{3,2},{4,5},{5,4},{6,7},{7,6},{8,9},{9,8},{10,11... | collective-permute-start | bytes 3145736 | tf_op jit(solution)/shard_map/ppermute | solution.py:223
  39.4 26.4 %all-to-all-start.2 = ((bf16[16,136,128]{2,1,0:T(8,128)(2,1)}), bf16[16,136,128]{2,1,0:T(8,128)(2,1)S(1)}, u32[]{:S(2)}, u32[]{:S(2)}) async-start(bf16[16,136,128]{2,1,0:T(8,128)(2,1)} %shard_map.105), calls=%async_computation.2 | async-start | bytes 1114112 | tf_op jit(solution)/shard_map/all_to_all | solution.py:245
  68.9 24.7 %copy-start.3 = (bf16[512,512]{1,0:T(8,128)(2,1)S(1)}, bf16[512,512]{1,0:T(8,128)(2,1)}, u32[]{:S(2)}) copy-start(bf16[512,512]{1,0:T(8,128)(2,1)} %copy-done.2) | copy-start | bytes 1572868
  91.0 3.7 %copy-start.6 = (bf16[512,512]{1,0:T(8,128)(2,1)S(1)}, bf16[512,512]{1,0:T(8,128)(2,1)}, u32[]{:S(2)}) copy-start(bf16[512,512]{1,0:T(8,128)(2,1)} %copy-done.5) | copy-start | bytes 1572868
  91.0 4.1 %collective-permute-start.3 = (bf16[512,512]{1,0:T(8,128)(2,1)S(1)}, bf16[512,512]{1,0:T(8,128)(2,1)S(1)}, u32[]{:S(2)}, u32[]{:S(2)}) collective-permute-start(bf16[512,512]{1,0:T(8,128)(2,1)S(1)} %bitcast.13), channel_id=1, source_target_pairs={{0,1},{1,0},{2,3},{3,2},{4,5},{5,4},{6,7},{7,6},{8,9},{9,8},{10,11... | collective-permute-start | bytes 1572872 | tf_op jit(solution)/shard_map/ppermute | solution.py:223

commit v4 on v3

--- a/solution.py
+++ b/solution.py
@@ -19,7 +19,7 @@
 BF16 = jnp.bfloat16
 VMEM = pl.BlockSpec(memory_space=pltpu.VMEM)
 STAT_ROWS = 8
-ORDER = tuple(2 * z + y for y in range(2) for z in range(8))
+ORDER = (9, 11, 13, 15, 1, 3, 5, 7, 8, 10, 12, 14, 0, 2, 4, 6)
 
 
 def nn(a, b):
@@ -30,14 +30,14 @@
     return lax.dot_general(a, b, (((1,), (1,)), ((), ())), preferred_element_type=F32)
 
 
-def call(kernel, out_shape, args, scratch=(), flops=1 << 20, transcendentals=0, left=0):
+def call(kernel, out_shape, args, scratch=(), flops=1 << 20, transcendentals=0):
     single = isinstance(out_shape, jax.ShapeDtypeStruct)
     outs = (out_shape,) if single else tuple(out_shape)
     moved = sum(a.size * a.dtype.itemsize for a in (*args, *outs))
     return pl.pallas_call(
         kernel,
         out_shape=out_shape,
-        in_specs=[VMEM] * (len(args) - left) + [pl.BlockSpec(memory_space=pltpu.HBM)] * left,
+        in_specs=[VMEM] * len(args),
         out_specs=VMEM if single else tuple([VMEM] * len(outs)),
         scratch_shapes=list(scratch),
         compiler_params=pltpu.CompilerParams(vmem_limit_bytes=16 << 20),
@@ -54,21 +54,10 @@
     return jnp.where(col == source, 1.0, 0.0).astype(BF16)
 
 
-def by_position_kernel(
-    frames, positions, x_ref, gain_ref, moe_ref, o_ref, gain_out, moe_out, back_ref, x_s, sems
-):
-    copies = (
-        pltpu.make_async_copy(x_ref, x_s, sems.at[0]),
-        pltpu.make_async_copy(gain_ref, gain_out, sems.at[1]),
-        pltpu.make_async_copy(moe_ref, moe_out, sems.at[2]),
-    )
-    for copy in copies:
-        copy.start()
-    order = one_hot(frames * positions, positions, frames)
-    back_ref[...] = one_hot(frames * positions, frames, positions)
-    for copy in copies:
-        copy.wait()
-    o_ref[...] = nn(order, x_s[...]).astype(BF16)
+def by_position_kernel(frames, positions, x_ref, gain_ref, moe_ref, o_ref, gain_out, moe_out):
+    gain_out[...] = gain_ref[...]
+    moe_out[...] = moe_ref[...]
+    o_ref[...] = nn(one_hot(frames * positions, positions, frames), x_ref[...]).astype(BF16)
 
 
 def rms(rows, gain):
@@ -117,7 +106,10 @@
     m_ref[...] = rms(r.astype(F32), gain_ref[...])
 
 
-def keys_kernel(keys_ref, slots_ref):
+def keys_kernel(frames, positions, keys_ref, r_ref, m_ref, slots_ref, r_out, m_out):
+    order = one_hot(frames * positions, frames, positions)
+    r_out[...] = nn(order, r_ref[...]).astype(BF16)
+    m_out[...] = nn(order, m_ref[...]).astype(BF16)
     half = SLOTS // 2
     core = lax.rem(lax.axis_index("pos"), 2)
     row = lax.broadcasted_iota(jnp.int32, (128, 256), 0)
@@ -213,10 +205,9 @@
     o_ref[...] = r_ref[...].astype(F32) + nn(c_ref[:, :count], own_ref[...])
 
 
-def output_kernel(sum_ref, c_ref, other_ref, back_ref, o_ref):
+def output_kernel(sum_ref, c_ref, other_ref, o_ref):
     count = other_ref.shape[0]
-    out = (sum_ref[...] + nn(c_ref[:, count:], other_ref[...])).astype(BF16)
-    o_ref[...] = nn(back_ref[...], out).astype(BF16)
+    o_ref[...] = (sum_ref[...] + nn(c_ref[:, count:], other_ref[...])).astype(BF16)
 
 
 def from_other_core(block):
@@ -236,6 +227,9 @@
     def by_position(*refs):
         by_position_kernel(frame_count, pos_count, *refs)
 
+    def keys(*refs):
+        keys_kernel(frame_count, pos_count, *refs)
+
     def over_frames(block):
         block = block.reshape(pos_count, frame_count, features)
         block = lax.all_to_all(block, "frame", split_axis=0, concat_axis=0, tiled=True)
@@ -249,34 +243,34 @@
     other_in = from_other_core(w_in[0])
     other_out = from_other_core(w_out[0])
     line = jax.ShapeDtypeStruct((1, features), F32)
-    x, gain, gain_moe, back = call(
+    x, gain, gain_moe = call(
         by_position,
-        (wide, line, line, jax.ShapeDtypeStruct((tokens, tokens), BF16)),
+        (wide, line, line),
         (frames_in.reshape(tokens, features), attn_gain.reshape(1, -1), moe_gain.reshape(1, -1)),
-        scratch=[pltpu.VMEM((tokens, features), BF16), pltpu.SemaphoreType.DMA((3,))],
-        left=3,
         flops=2 * tokens**2 * features,
     )
+    spread = over_frames(x)
     mixed = call(
         attention_kernel,
         wide,
-        (over_frames(x), gain, w_query, w_key, w_value),
+        (spread, gain, w_query, w_key, w_value),
         scratch=[pltpu.VMEM((tokens, features), BF16)] * 4 + [pltpu.VMEM((tokens, tokens), BF16)],
         flops=14 * tokens**2 * features,
         transcendentals=HEADS * tokens**2,
     )
+    mixed = over_frames(mixed)
     residual, moe_input = call(
         residual_kernel,
         (wide, wide),
-        (over_frames(mixed), x, w_output, gain_moe),
+        (mixed, x, w_output, gain_moe),
         flops=2 * tokens**2 * features,
     )
     other_input = from_other_core(moe_input)
-    slot_keys = call(
-        keys_kernel,
-        jax.ShapeDtypeStruct((EXPERTS * SLOTS, features), BF16),
-        (dispatch_keys,),
-        flops=512 * tokens * features,
+    slot_keys, residual, ordered_input = call(
+        keys,
+        (jax.ShapeDtypeStruct((EXPERTS * SLOTS, features), BF16), wide, wide),
+        (dispatch_keys, residual, moe_input),
+        flops=512 * tokens * features + 4 * tokens**2 * features,
     )
     sums = call(
         dispatch_kernel,
@@ -298,7 +292,7 @@
     combine = call(
         combine_kernel,
         jax.ShapeDtypeStruct((tokens, EXPERTS * SLOTS), BF16),
-        (moe_input, slot_keys),
+        (ordered_input, slot_keys),
         flops=4 * tokens**2 * features,
         transcendentals=2 * tokens**2,
     )
@@ -309,7 +303,7 @@
         flops=2 * tokens**2 * features,
     )
     out = call(
-        output_kernel, wide, (own_sum, combine, other_half, back), flops=4 * tokens**2 * features
+        output_kernel, wide, (own_sum, combine, other_half), flops=2 * tokens**2 * features
     )
     return out.reshape(frame_count, pos_count, features)
 

time: 97.2 us -> 95.7 us (0.985)
  waiting for transfers between devices: 16 us -> 13.6 us
  local copies, waits for them, and re-layouts: 1.79 us -> 3.55 us
    all_to_all x1, waiting for transfers between devices: 15.8 us -> 13.5 us  [over_chips(): lax.all_to_all(blocks, 'pos', split_axis=0, concat_axis=0, tiled=True, ax...]
    all_to_all x1, starting transfers between devices: 10.6 us -> 12.7 us  [over_chips(): lax.all_to_all(blocks, 'pos', split_axis=0, concat_axis=0, tiled=True, ax...]
    unnamed x26 -> x28, local copies, waits for them, and re-layouts: 1.79 us -> 3.55 us
    ppermute x4, starting transfers between devices: 6.6 us -> 5.07 us  [from_other_core(): lax.ppermute(block, 'pos', [(k, k ^ 1) for k in range(lax.axis_size('pos'...]
  transfers between devices with their start and end apart: 5 -> 5, of which waited for: 2 -> 1; matrix products, arithmetic and copies ran while one was open for 0% -> 0% of each run, Pallas kernels for 5% -> 6%
where the time goes in v4:
time: 95.7 us; the launch traced here: 95.3 us
  blocking collectives  46 us (48%)
  starting transfers between devices  17.8 us (19%)
  Pallas kernels  14.2 us (15%)
  waiting for transfers between devices  13.6 us (14%)
  local copies, waits for them, and re-layouts  3.55 us (4%)
    all_to_all x2, blocking collectives, over_frames(): lax.all_to_all(block, 'frame', split_axis=0, concat_axis=0, tiled=True)  24.7 us
    all_to_all x1, blocking collectives, over_chips(): lax.all_to_all(blocks, 'pos', split_axis=0, concat_axis=0, tiled=True, ax...  21.3 us
    pallas_call x9, Pallas kernels, call(): pl.pallas_call(kernel, out_shape=out_shape, in_specs=[VMEM] * len(args),...  14.2 us
    all_to_all x1, waiting for transfers between devices, over_chips(): lax.all_to_all(blocks, 'pos', split_axis=0, concat_axis=0, tiled=True, ax...  13.5 us
    all_to_all x1, starting transfers between devices, over_chips(): lax.all_to_all(blocks, 'pos', split_axis=0, concat_axis=0, tiled=True, ax...  12.7 us
    ppermute x4, starting transfers between devices, from_other_core(): lax.ppermute(block, 'pos', [(k, k ^ 1) for k in range(lax.axis_size('pos'...  5.07 us
    unnamed x28, local copies, waits for them, and re-layouts  3.55 us
  transfers between devices with their start and end apart: 5, of which 1 were waited for; matrix products, arithmetic and copies ran while one was open for 0% of the time, Pallas kernels for 6%

profile of v4, /device:TPU:1, one launch (start us, length us, event | category | flops | bytes accessed | tf_op | source)
XLA Modules:
  0.0 95.3 jit_solution(6133048009547752898)
XLA Ops:
  0.0 0.7 copy-done.13
  0.7 0.0 copy-done.12
  0.7 1.0 %copy-done.8 = bf16[64,8,512]{2,1,0:T(8,128)(2,1)S(1)} copy-done((bf16[64,8,512]{2,1,0:T(8,128)(2,1)S(1)}, bf16[64,8,512]{2,1,0:T(8,128)(2,1)}, u32[]{:S(2)}) %copy-start.8) | copy-done | bytes 524312
  1.7 0.4 shard_map.100
  2.2 0.0 copy-start.9
  2.2 0.0 copy-start.10
  2.2 14.4 %all_to_all.20 = bf16[8,64,512]{2,1,0:T(8,128)(2,1)S(1)} all-to-all(bf16[8,64,512]{2,1,0:T(8,128)(2,1)S(1)} %bitcast.11), channel_id=1, replica_groups=mesh['frame'=8,'pos'=32] {'frame'}, dimensions={0} | all-to-all | bytes 1048576 | tf_op jit(solution)/shard_map/all_to_all | solution.py:235
  16.7 0.0 copy-start.4
  16.7 0.0 copy-start.7
  16.7 3.8 %shard_map.101 = bf16[512,512]{1,0:T(8,128)(2,1)S(1)} custom-call(bf16[512,512]{1,0:T(8,128)(2,1)S(1)} %bitcast.20, f32[1,512]{1,0:T(1,128)S(1)} %get-tuple-element.14.gain_ref, bf16[512,512]{1,0:T(8,128)(2,1)S(1)} %copy-done.9, bf16[512,512]{1,0:T(8,128)(2,1)S(1)} %copy-done.10, bf16[512,512]{1,0:T(8,128)(2,1)S(1)} %copy-done.11), custom_call_target="tpu_custom_call" | custom-call | flops 1879048192 | bytes 2623488 | tf_op jit(solution)/shard_map/pallas_call | solution.py:37
  20.4 0.0 copy-start.1
  20.5 10.3 %all_to_all.21 = bf16[8,64,512]{2,1,0:T(8,128)(2,1)S(1)} all-to-all(bf16[8,64,512]{2,1,0:T(8,128)(2,1)S(1)} %bitcast.19), channel_id=1, replica_groups=mesh['frame'=8,'pos'=32] {'frame'}, dimensions={0} | all-to-all | bytes 1048576 | tf_op jit(solution)/shard_map/all_to_all | solution.py:235
  30.7 0.7 shard_map.102
  31.4 3.5 %collective-permute-start = (bf16[512,512]{1,0:T(8,128)(2,1)S(1)}, bf16[512,512]{1,0:T(8,128)(2,1)S(1)}, u32[]{:S(2)}, u32[]{:S(2)}) collective-permute-start(bf16[512,512]{1,0:T(8,128)(2,1)S(1)} %get-tuple-element.17.refs_2_.m_ref), channel_id=1, source_target_pairs={{0,1},{1,0},{2,3},{3,2},{4,5},{5,4},{6,7},{7,6},{8,9},{9,8},{10,11... | collective-permute-start | bytes 1572872 | tf_op jit(solution)/shard_map/ppermute | solution.py:214
  34.9 0.5 collective-permute-start.1
  35.4 0.0 collective-permute-start.2
  35.5 1.3 %shard_map.103 = (bf16[1024,512]{1,0:T(8,128)(2,1)S(1)}, bf16[512,512]{1,0:T(8,128)(2,1)S(1)}, bf16[512,512]{1,0:T(8,128)(2,1)S(1)}) custom-call(bf16[512,1024]{1,0:T(8,128)(2,1)S(1)} %copy-done.7, bf16[512,512]{1,0:T(8,128)(2,1)S(1)} %get-tuple-element.16.refs_1_, bf16[512,512]{1,0:T(8,128)(2,1)S(1)} %get-tuple-element.17.refs_2_.m_ref), custom_call_target="tpu_custom_call" | custom-call | flops 671088640 | bytes 4194304 | tf_op jit(solution)/shard_map/pallas_call | solution.py:37
  36.8 0.0 copy-start.5
  36.8 0.8 copy-done.5
  37.6 0.0 collective-permute-done.other_ref
  37.6 2.6 %shard_map.105 = bf16[16,136,128]{2,1,0:T(8,128)(2,1)} custom-call(bf16[512,512]{1,0:T(8,128)(2,1)S(1)} %get-tuple-element.17.refs_2_.m_ref, bf16[512,512]{1,0:T(8,128)(2,1)S(1)} %collective-permute-done.other_ref, bf16[1024,512]{1,0:T(8,128)(2,1)S(1)} %get-tuple-element.20.slots_ref.keys_ref), custom_call_target="tpu_custom_call" | custom-call | flops 1073741824 | bytes 2654208 | tf_op jit(solution)/shard_map/pallas_call | solution.py:37
  40.2 1.0 %copy-done.2 = bf16[1024,512]{1,0:T(8,128)(2,1)} copy-done((bf16[1024,512]{1,0:T(8,128)(2,1)}, bf16[1024,512]{1,0:T(8,128)(2,1)S(1)}, u32[]{:S(2)}) %copy-start.2) | copy-done | bytes 1048600
  41.1 12.7 %all-to-all-start.2 = ((bf16[16,136,128]{2,1,0:T(8,128)(2,1)}), bf16[16,136,128]{2,1,0:T(8,128)(2,1)S(1)}, u32[]{:S(2)}, u32[]{:S(2)}) async-start(bf16[16,136,128]{2,1,0:T(8,128)(2,1)} %shard_map.105), calls=%async_computation.2 | async-start | bytes 1114112 | tf_op jit(solution)/shard_map/all_to_all | solution.py:239
  53.8 0.0 collective-permute-done.2.other_out_ref
  53.9 13.5 %all-to-all-done.2.got_ref = bf16[16,136,128]{2,1,0:T(8,128)(2,1)S(1)} async-done(((bf16[16,136,128]{2,1,0:T(8,128)(2,1)}), bf16[16,136,128]{2,1,0:T(8,128)(2,1)S(1)}, u32[]{:S(2)}, u32[]{:S(2)}) %all-to-all-start.2) | async-done | bytes 557088 | tf_op jit(solution)/shard_map/all_to_all | solution.py:239
  67.4 2.7 %shard_map.106 = bf16[16,32,512]{2,1,0:T(8,128)(2,1)S(1)} custom-call(bf16[16,136,128]{2,1,0:T(8,128)(2,1)S(1)} %all-to-all-done.2.got_ref, bf16[512,1024]{1,0:T(8,128)(2,1)S(1)} %bitcast.16, bf16[512,1024]{1,0:T(8,128)(2,1)} %collective-permute-done.1.other_in_ref, bf16[1024,512]{1,0:T(8,128)(2,1)S(1)} %bitcast.18, ...), custom_call_target="tpu_custom_call" | custom-call | flops 268435456 | bytes 5275648 | tf_op jit(solution)/shard_map/pallas_call | solution.py:37
  70.1 21.3 %all_to_all.22 = bf16[16,32,512]{2,1,0:T(8,128)(2,1)S(1)} all-to-all(bf16[16,32,512]{2,1,0:T(8,128)(2,1)S(1)} %shard_map.106), channel_id=1, replica_groups={{18,22,26,30,2,6,10,14,16,20,24,28,0,4,8,12},{19,23,27,31,3,7,11,15,17,..., dimensions={0} | all-to-all | bytes 1048576 | tf_op jit(solution)/shard_map/all_to_all | solution.py:239
  91.4 1.0 %collective-permute-start.3 = (bf16[512,512]{1,0:T(8,128)(2,1)S(1)}, bf16[512,512]{1,0:T(8,128)(2,1)S(1)}, u32[]{:S(2)}, u32[]{:S(2)}) collective-permute-start(bf16[512,512]{1,0:T(8,128)(2,1)S(1)} %bitcast.13), channel_id=1, source_target_pairs={{0,1},{1,0},{2,3},{3,2},{4,5},{5,4},{6,7},{7,6},{8,9},{9,8},{10,11... | collective-permute-start | bytes 1572872 | tf_op jit(solution)/shard_map/ppermute | solution.py:214
  92.5 1.1 %shard_map.104.c_ref = bf16[512,1024]{1,0:T(8,128)(2,1)S(1)} custom-call(bf16[512,512]{1,0:T(8,128)(2,1)S(1)} %get-tuple-element.19.m_ref, bf16[1024,512]{1,0:T(8,128)(2,1)S(1)} %copy-done.3), custom_call_target="tpu_custom_call" | custom-call | flops 536870912 | bytes 2621440 | tf_op jit(solution)/shard_map/pallas_call | solution.py:37
  93.6 0.4 shard_map.107.sum_ref
  94.0 0.0 collective-permute-done.3.other_ref
  94.0 1.2 %shard_map.108 = bf16[512,512]{1,0:T(8,128)(2,1)} custom-call(f32[512,512]{1,0:T(8,128)S(1)} %shard_map.107.sum_ref, bf16[512,1024]{1,0:T(8,128)(2,1)S(1)} %shard_map.104.c_ref, bf16[512,512]{1,0:T(8,128)(2,1)S(1)} %collective-permute-done.3.other_ref), custom_call_target="tpu_custom_call" | custom-call | flops 268435456 | bytes 3145728 | tf_op jit(solution)/shard_map/pallas_call | solution.py:37
  (18 shorter events, 0.0 us)
Async XLA Ops:
  0.0 0.7 copy-start.13
  0.0 0.7 copy-start.12
  0.7 1.0 %copy-start.8 = (bf16[64,8,512]{2,1,0:T(8,128)(2,1)S(1)}, bf16[64,8,512]{2,1,0:T(8,128)(2,1)}, u32[]{:S(2)}) copy-start(bf16[64,8,512]{2,1,0:T(8,128)(2,1)} %param.10) | copy-start | bytes 1572868
  1.7 14.9 %copy-start.11 = (bf16[512,512]{1,0:T(8,128)(2,1)S(1)}, bf16[512,512]{1,0:T(8,128)(2,1)}, u32[]{:S(2)}) copy-start(bf16[512,512]{1,0:T(8,128)(2,1)} %wv_ref.1) | copy-start | bytes 1572868
  2.2 14.5 %copy-start.9 = (bf16[512,512]{1,0:T(8,128)(2,1)S(1)}, bf16[512,512]{1,0:T(8,128)(2,1)}, u32[]{:S(2)}) copy-start(bf16[512,512]{1,0:T(8,128)(2,1)} %wq_ref.1) | copy-start | bytes 1572868
  2.2 14.5 %copy-start.10 = (bf16[512,512]{1,0:T(8,128)(2,1)S(1)}, bf16[512,512]{1,0:T(8,128)(2,1)}, u32[]{:S(2)}) copy-start(bf16[512,512]{1,0:T(8,128)(2,1)} %wk_ref.1) | copy-start | bytes 1572868
  16.7 14.1 %copy-start.4 = (bf16[512,512]{1,0:T(8,128)(2,1)S(1)}, bf16[512,512]{1,0:T(8,128)(2,1)}, u32[]{:S(2)}) copy-start(bf16[512,512]{1,0:T(8,128)(2,1)} %wo_ref.1) | copy-start | bytes 1572868
  16.7 18.8 %copy-start.7 = (bf16[512,1024]{1,0:T(8,128)(2,1)S(1)}, bf16[512,1024]{1,0:T(8,128)(2,1)}, u32[]{:S(2)}) copy-start(bf16[512,1024]{1,0:T(8,128)(2,1)} %refs_0_.1) | copy-start | bytes 3145732
  20.4 15.0 %copy-start.1 = (bf16[1,1024,512]{2,1,0:T(8,128)(2,1)S(1)}, bf16[1,1024,512]{2,1,0:T(8,128)(2,1)}, u32[]{:S(2)}) copy-start(bf16[1,1024,512]{2,1,0:T(8,128)(2,1)} %param.19) | copy-start | bytes 3145732
  30.7 4.2 %copy-start = (bf16[1,512,1024]{2,1,0:T(8,128)(2,1)S(1)}, bf16[1,512,1024]{2,1,0:T(8,128)(2,1)}, u32[]{:S(2)}) copy-start(bf16[1,512,1024]{2,1,0:T(8,128)(2,1)} %param.18) | copy-start | bytes 3145732
  31.4 6.2 %collective-permute-start = (bf16[512,512]{1,0:T(8,128)(2,1)S(1)}, bf16[512,512]{1,0:T(8,128)(2,1)S(1)}, u32[]{:S(2)}, u32[]{:S(2)}) collective-permute-start(bf16[512,512]{1,0:T(8,128)(2,1)S(1)} %get-tuple-element.17.refs_2_.m_ref), channel_id=1, source_target_pairs={{0,1},{1,0},{2,3},{3,2},{4,5},{5,4},{6,7},{7,6},{8,9},{9,8},{10,11... | collective-permute-start | bytes 1572872 | tf_op jit(solution)/shard_map/ppermute | solution.py:214
  34.9 18.9 %collective-permute-start.1 = (bf16[512,1024]{1,0:T(8,128)(2,1)S(1)}, bf16[512,1024]{1,0:T(8,128)(2,1)}, u32[]{:S(2)}, u32[]{:S(2)}) collective-permute-start(bf16[512,1024]{1,0:T(8,128)(2,1)S(1)} %bitcast.15), channel_id=1, source_target_pairs={{0,1},{1,0},{2,3},{3,2},{4,5},{5,4},{6,7},{7,6},{8,9},{9,8},{10,11... | collective-permute-start | bytes 3145736 | tf_op jit(solution)/shard_map/ppermute | solution.py:214
  35.4 18.4 %collective-permute-start.2 = (bf16[1024,512]{1,0:T(8,128)(2,1)S(1)}, bf16[1024,512]{1,0:T(8,128)(2,1)}, u32[]{:S(2)}, u32[]{:S(2)}) collective-permute-start(bf16[1024,512]{1,0:T(8,128)(2,1)S(1)} %bitcast.17), channel_id=1, source_target_pairs={{0,1},{1,0},{2,3},{3,2},{4,5},{5,4},{6,7},{7,6},{8,9},{9,8},{10,11... | collective-permute-start | bytes 3145736 | tf_op jit(solution)/shard_map/ppermute | solution.py:214
  36.8 0.8 copy-start.5
  40.2 1.0 %copy-start.2 = (bf16[1024,512]{1,0:T(8,128)(2,1)}, bf16[1024,512]{1,0:T(8,128)(2,1)S(1)}, u32[]{:S(2)}) copy-start(bf16[1024,512]{1,0:T(8,128)(2,1)S(1)} %get-tuple-element.20.slots_ref.keys_ref) | copy-start | bytes 3145732
  41.1 26.3 %all-to-all-start.2 = ((bf16[16,136,128]{2,1,0:T(8,128)(2,1)}), bf16[16,136,128]{2,1,0:T(8,128)(2,1)S(1)}, u32[]{:S(2)}, u32[]{:S(2)}) async-start(bf16[16,136,128]{2,1,0:T(8,128)(2,1)} %shard_map.105), calls=%async_computation.2 | async-start | bytes 1114112 | tf_op jit(solution)/shard_map/all_to_all | solution.py:239
  70.1 22.4 %copy-start.3 = (bf16[1024,512]{1,0:T(8,128)(2,1)S(1)}, bf16[1024,512]{1,0:T(8,128)(2,1)}, u32[]{:S(2)}) copy-start(bf16[1024,512]{1,0:T(8,128)(2,1)} %copy-done.2) | copy-start | bytes 3145732
  91.4 2.6 %collective-permute-start.3 = (bf16[512,512]{1,0:T(8,128)(2,1)S(1)}, bf16[512,512]{1,0:T(8,128)(2,1)S(1)}, u32[]{:S(2)}, u32[]{:S(2)}) collective-permute-start(bf16[512,512]{1,0:T(8,128)(2,1)S(1)} %bitcast.13), channel_id=1, source_target_pairs={{0,1},{1,0},{2,3},{3,2},{4,5},{5,4},{6,7},{7,6},{8,9},{9,8},{10,11... | collective-permute-start | bytes 1572872 | tf_op jit(solution)/shard_map/ppermute | solution.py:214
  92.5 1.1 %copy-start.6 = (bf16[512,512]{1,0:T(8,128)(2,1)S(1)}, bf16[512,512]{1,0:T(8,128)(2,1)}, u32[]{:S(2)}) copy-start(bf16[512,512]{1,0:T(8,128)(2,1)} %copy-done.5) | copy-start | bytes 1572868

commit v5 on v4

--- a/solution.py
+++ b/solution.py
@@ -20,6 +20,8 @@
 VMEM = pl.BlockSpec(memory_space=pltpu.VMEM)
 STAT_ROWS = 8
 ORDER = (9, 11, 13, 15, 1, 3, 5, 7, 8, 10, 12, 14, 0, 2, 4, 6)
+BACK = ORDER
+FRAMES = (5, 7, 4, 6, 3, 2, 1, 0)
 
 
 def nn(a, b):
@@ -68,7 +70,11 @@
 def attention_kernel(x_ref, gain_ref, wq_ref, wk_ref, wv_ref, o_ref, n_s, q_s, k_s, v_s, w_s):
     frames, features = x_ref.shape
     head_dim = features // HEADS
-    n_s[...] = rms(x_ref[...].astype(F32), gain_ref[...])
+    run = frames // len(FRAMES)
+    for i, place in enumerate(FRAMES):
+        n_s[place * run : (place + 1) * run, :] = rms(
+            x_ref[i * run : (i + 1) * run, :].astype(F32), gain_ref[...]
+        )
     q_s[...] = (nn(n_s[...], wq_ref[...]) * (head_dim ** (-0.5) * LOG2E)).astype(BF16)
     k_s[...] = nn(n_s[...], wk_ref[...]).astype(BF16)
     v_s[...] = nn(n_s[...], wv_ref[...]).astype(BF16)
@@ -97,7 +103,9 @@
             v = jnp.where(mine, v_s[:, lanes], jnp.ones((), BF16))
             mixed.append(nn(w_s[...], v))
         total = pltpu.roll(jnp.where(low, mixed[1], mixed[0]), head_dim, 1)
-        o_ref[:, lanes] = (jnp.where(low, mixed[0], mixed[1]) / total).astype(BF16)
+        out = (jnp.where(low, mixed[0], mixed[1]) / total).astype(BF16)
+        for i, place in enumerate(FRAMES):
+            o_ref[i * run : (i + 1) * run, lanes] = out[place * run : (place + 1) * run, :]
 
 
 def residual_kernel(mixed_ref, x_ref, wo_ref, gain_ref, r_ref, m_ref):
@@ -106,7 +114,7 @@
     m_ref[...] = rms(r.astype(F32), gain_ref[...])
 
 
-def keys_kernel(frames, positions, keys_ref, r_ref, m_ref, slots_ref, r_out, m_out):
+def keys_kernel(frames, positions, keys_ref, r_ref, m_ref, own_ref, slots_ref, r_out, m_out):
     order = one_hot(frames * positions, frames, positions)
     r_out[...] = nn(order, r_ref[...]).astype(BF16)
     m_out[...] = nn(order, m_ref[...]).astype(BF16)
@@ -122,8 +130,13 @@
         for k in range(count // 128):
             keys = nt(pick, keys_ref[:, 256 * k : 256 * k + 256]).astype(BF16)
             for i in range(128 // half):
-                at = turn * count + half * ORDER.index(k * (128 // half) + i)
-                slots_ref[at : at + half, :] = keys[i * half : (i + 1) * half, :]
+                chip = k * (128 // half) + i
+                rows = keys[i * half : (i + 1) * half, :]
+                at = turn * count + half * BACK.index(chip)
+                slots_ref[at : at + half, :] = rows
+                if turn == 0:
+                    at = half * ORDER.index(chip)
+                    own_ref[at : at + half, :] = rows
 
 
 def combine_kernel(m_ref, slots_ref, c_ref):
@@ -141,7 +154,7 @@
     all_s[tokens:, :] = other_ref[...]
     half = SLOTS // 2
     rows = 256
-    for start in range(0, keys_ref.shape[0] // 2, rows):
+    for start in range(0, keys_ref.shape[0], rows):
         t = nt(keys_ref[start : start + rows, :], all_s[...]) * (LOGIT_SCALE * LOG2E)
         largest = jnp.max(t, axis=1, keepdims=True)
         w = jnp.exp2(t - largest)
@@ -221,7 +234,6 @@
     tokens = frame_count * pos_count
     chips = lax.axis_size("pos") // 2
     half = SLOTS // 2
-    by_core = [[2 * chip + core for chip in ORDER] for core in range(2)]
     wide = jax.ShapeDtypeStruct((tokens, features), BF16)
 
     def by_position(*refs):
@@ -232,10 +244,13 @@
 
     def over_frames(block):
         block = block.reshape(pos_count, frame_count, features)
-        block = lax.all_to_all(block, "frame", split_axis=0, concat_axis=0, tiled=True)
+        block = lax.all_to_all(
+            block, "frame", split_axis=0, concat_axis=0, tiled=True, axis_index_groups=[list(FRAMES)]
+        )
         return block.reshape(tokens, features)
 
-    def over_chips(blocks):
+    def over_chips(blocks, order):
+        by_core = [[2 * chip + core for chip in order] for core in range(2)]
         return lax.all_to_all(
             blocks, "pos", split_axis=0, concat_axis=0, tiled=True, axis_index_groups=by_core
         )
@@ -266,16 +281,21 @@
         flops=2 * tokens**2 * features,
     )
     other_input = from_other_core(moe_input)
-    slot_keys, residual, ordered_input = call(
+    own_keys, slot_keys, residual, ordered_input = call(
         keys,
-        (jax.ShapeDtypeStruct((EXPERTS * SLOTS, features), BF16), wide, wide),
+        (
+            jax.ShapeDtypeStruct((chips * half, features), BF16),
+            jax.ShapeDtypeStruct((2 * chips * half, features), BF16),
+            wide,
+            wide,
+        ),
         (dispatch_keys, residual, moe_input),
         flops=512 * tokens * features + 4 * tokens**2 * features,
     )
     sums = call(
         dispatch_kernel,
         jax.ShapeDtypeStruct((chips, features // 128 * half + STAT_ROWS, 128), BF16),
-        (moe_input, other_input, slot_keys),
+        (moe_input, other_input, own_keys),
         scratch=[pltpu.VMEM((2 * tokens, features), BF16)],
         flops=8 * tokens**2 * features,
         transcendentals=2 * tokens**2,
@@ -283,11 +303,11 @@
     outputs = call(
         expert_kernel,
         jax.ShapeDtypeStruct((chips, half, features), BF16),
-        (over_chips(sums), w_in[0], other_in, w_out[0], other_out),
+        (over_chips(sums, ORDER), w_in[0], other_in, w_out[0], other_out),
         scratch=[pltpu.VMEM((128, 128), F32)],
         flops=16 * SLOTS * features**2,
     )
-    own_half = over_chips(outputs).reshape(-1, features)
+    own_half = over_chips(outputs, BACK).reshape(-1, features)
     other_half = from_other_core(own_half)
     combine = call(
         combine_kernel,

time: 95.7 us -> 94.2 us (0.984)
    ppermute x4, starting transfers between devices: 5.07 us -> 3.73 us  [from_other_core(): lax.ppermute(block, 'pos', [(k, k ^ 1) for k in range(lax.axis_size('pos'...]
where the time goes in v5:
time: 94.2 us; the launch traced here: 93.8 us
  blocking collectives  45.3 us (48%)
  starting transfers between devices  17 us (18%)
  Pallas kernels  14.2 us (15%)
  waiting for transfers between devices  13.6 us (14%)
  local copies, waits for them, and re-layouts  3.57 us (4%)
    all_to_all x2, blocking collectives, over_frames(): lax.all_to_all(block, 'frame', split_axis=0, concat_axis=0, tiled=True, a...  24 us
    all_to_all x1, blocking collectives, over_chips(): lax.all_to_all(blocks, 'pos', split_axis=0, concat_axis=0, tiled=True, ax...  21.3 us
    pallas_call x9, Pallas kernels, call(): pl.pallas_call(kernel, out_shape=out_shape, in_specs=[VMEM] * len(args),...  14.2 us
    all_to_all x1, waiting for transfers between devices, over_chips(): lax.all_to_all(blocks, 'pos', split_axis=0, concat_axis=0, tiled=True, ax...  13.5 us
    all_to_all x1, starting transfers between devices, over_chips(): lax.all_to_all(blocks, 'pos', split_axis=0, concat_axis=0, tiled=True, ax...  13.3 us
    ppermute x4, starting transfers between devices, from_other_core(): lax.ppermute(block, 'pos', [(k, k ^ 1) for k in range(lax.axis_size('pos'...  3.73 us
    unnamed x28, local copies, waits for them, and re-layouts  3.57 us
  transfers between devices with their start and end apart: 5, of which 1 were waited for; matrix products, arithmetic and copies ran while one was open for 0% of the time, Pallas kernels for 6%

profile of v5, /device:TPU:1, one launch (start us, length us, event | category | flops | bytes accessed | tf_op | source)
XLA Modules:
  0.0 93.8 jit_solution(9843867165472081995)
XLA Ops:
  0.0 0.7 copy-done.13
  0.7 0.0 copy-done.12
  0.7 1.0 %copy-done.8 = bf16[64,8,512]{2,1,0:T(8,128)(2,1)S(1)} copy-done((bf16[64,8,512]{2,1,0:T(8,128)(2,1)S(1)}, bf16[64,8,512]{2,1,0:T(8,128)(2,1)}, u32[]{:S(2)}) %copy-start.8) | copy-done | bytes 524312
  1.7 0.4 shard_map.100
  2.2 0.0 copy-start.9
  2.2 0.0 copy-start.10
  2.2 12.8 %all_to_all.20 = bf16[8,64,512]{2,1,0:T(8,128)(2,1)S(1)} all-to-all(bf16[8,64,512]{2,1,0:T(8,128)(2,1)S(1)} %bitcast.11), channel_id=1, replica_groups={{160,224,128,192,96,64,32,0},{161,225,129,193,97,65,33,1},{162,226,130,..., dimensions={0} | all-to-all | bytes 1048576 | tf_op jit(solution)/shard_map/all_to_all | solution.py:247
  15.0 0.0 copy-start.4
  15.0 0.0 copy-start.7
  15.0 3.7 %shard_map.101 = bf16[512,512]{1,0:T(8,128)(2,1)S(1)} custom-call(bf16[512,512]{1,0:T(8,128)(2,1)S(1)} %bitcast.20, f32[1,512]{1,0:T(1,128)S(1)} %get-tuple-element.15.gain_ref, bf16[512,512]{1,0:T(8,128)(2,1)S(1)} %copy-done.9, bf16[512,512]{1,0:T(8,128)(2,1)S(1)} %copy-done.10, bf16[512,512]{1,0:T(8,128)(2,1)S(1)} %copy-done.11), custom_call_target="tpu_custom_call" | custom-call | flops 1879048192 | bytes 2623488 | tf_op jit(solution)/shard_map/pallas_call | solution.py:39
  18.8 0.0 copy-start.1
  18.8 11.2 %all_to_all.21 = bf16[8,64,512]{2,1,0:T(8,128)(2,1)S(1)} all-to-all(bf16[8,64,512]{2,1,0:T(8,128)(2,1)S(1)} %bitcast.19), channel_id=1, replica_groups={{160,224,128,192,96,64,32,0},{161,225,129,193,97,65,33,1},{162,226,130,..., dimensions={0} | all-to-all | bytes 1048576 | tf_op jit(solution)/shard_map/all_to_all | solution.py:247
  30.0 0.7 shard_map.102
  30.6 2.2 %collective-permute-start = (bf16[512,512]{1,0:T(8,128)(2,1)S(1)}, bf16[512,512]{1,0:T(8,128)(2,1)S(1)}, u32[]{:S(2)}, u32[]{:S(2)}) collective-permute-start(bf16[512,512]{1,0:T(8,128)(2,1)S(1)} %get-tuple-element.18.refs_2_.m_ref), channel_id=1, source_target_pairs={{0,1},{1,0},{2,3},{3,2},{4,5},{5,4},{6,7},{7,6},{8,9},{9,8},{10,11... | collective-permute-start | bytes 1572872 | tf_op jit(solution)/shard_map/ppermute | solution.py:227
  32.8 0.5 collective-permute-start.1
  33.3 0.0 collective-permute-start.2
  33.3 1.3 %shard_map.103 = (bf16[512,512]{1,0:T(8,128)(2,1)S(1)}, bf16[1024,512]{1,0:T(8,128)(2,1)S(1)}, bf16[512,512]{1,0:T(8,128)(2,1)S(1)}, bf16[512,512]{1,0:T(8,128)(2,1)S(1)}) custom-call(bf16[512,1024]{1,0:T(8,128)(2,1)S(1)} %copy-done.7, bf16[512,512]{1,0:T(8,128)(2,1)S(1)} %get-tuple-element.17.refs_1_, bf16[512,512]{1,0:T(8,128)(2,1)S(1)} %get-tuple-element.18.refs_2_.m_ref), custom_call_target="tpu_custom_call" | custom-call | flops 671088640 | bytes 4718592 | tf_op jit(solution)/shard_map/pallas_call | solution.py:39
  34.7 1.0 %copy-done.2 = bf16[1024,512]{1,0:T(8,128)(2,1)} copy-done((bf16[1024,512]{1,0:T(8,128)(2,1)}, bf16[1024,512]{1,0:T(8,128)(2,1)S(1)}, u32[]{:S(2)}) %copy-start.2) | copy-done | bytes 1048600
  35.7 0.8 copy-done.5
  36.5 0.0 collective-permute-done.other_ref
  36.5 2.6 %shard_map.105 = bf16[16,136,128]{2,1,0:T(8,128)(2,1)} custom-call(bf16[512,512]{1,0:T(8,128)(2,1)S(1)} %get-tuple-element.18.refs_2_.m_ref, bf16[512,512]{1,0:T(8,128)(2,1)S(1)} %collective-permute-done.other_ref, bf16[512,512]{1,0:T(8,128)(2,1)S(1)} %get-tuple-element.22.keys_ref), custom_call_target="tpu_custom_call" | custom-call | flops 1073741824 | bytes 2129920 | tf_op jit(solution)/shard_map/pallas_call | solution.py:39
  39.0 13.3 %all-to-all-start.2 = ((bf16[16,136,128]{2,1,0:T(8,128)(2,1)}), bf16[16,136,128]{2,1,0:T(8,128)(2,1)S(1)}, u32[]{:S(2)}, u32[]{:S(2)}) async-start(bf16[16,136,128]{2,1,0:T(8,128)(2,1)} %shard_map.105), calls=%async_computation.2 | async-start | bytes 1114112 | tf_op jit(solution)/shard_map/all_to_all | solution.py:254
  52.3 0.0 collective-permute-done.1.other_in_ref
  52.3 0.0 collective-permute-done.2.other_out_ref
  52.3 13.5 %all-to-all-done.2.got_ref = bf16[16,136,128]{2,1,0:T(8,128)(2,1)S(1)} async-done(((bf16[16,136,128]{2,1,0:T(8,128)(2,1)}), bf16[16,136,128]{2,1,0:T(8,128)(2,1)S(1)}, u32[]{:S(2)}, u32[]{:S(2)}) %all-to-all-start.2) | async-done | bytes 557088 | tf_op jit(solution)/shard_map/all_to_all | solution.py:254
  65.9 2.7 %shard_map.106 = bf16[16,32,512]{2,1,0:T(8,128)(2,1)S(1)} custom-call(bf16[16,136,128]{2,1,0:T(8,128)(2,1)S(1)} %all-to-all-done.2.got_ref, bf16[512,1024]{1,0:T(8,128)(2,1)S(1)} %bitcast.16, bf16[512,1024]{1,0:T(8,128)(2,1)} %collective-permute-done.1.other_in_ref, bf16[1024,512]{1,0:T(8,128)(2,1)S(1)} %bitcast.18, ...), custom_call_target="tpu_custom_call" | custom-call | flops 268435456 | bytes 5275648 | tf_op jit(solution)/shard_map/pallas_call | solution.py:39
  68.6 21.3 %all_to_all.22 = bf16[16,32,512]{2,1,0:T(8,128)(2,1)S(1)} all-to-all(bf16[16,32,512]{2,1,0:T(8,128)(2,1)S(1)} %shard_map.106), channel_id=1, replica_groups={{18,22,26,30,2,6,10,14,16,20,24,28,0,4,8,12},{19,23,27,31,3,7,11,15,17,..., dimensions={0} | all-to-all | bytes 1048576 | tf_op jit(solution)/shard_map/all_to_all | solution.py:254
  89.9 1.0 %collective-permute-start.3 = (bf16[512,512]{1,0:T(8,128)(2,1)S(1)}, bf16[512,512]{1,0:T(8,128)(2,1)S(1)}, u32[]{:S(2)}, u32[]{:S(2)}) collective-permute-start(bf16[512,512]{1,0:T(8,128)(2,1)S(1)} %bitcast.13), channel_id=1, source_target_pairs={{0,1},{1,0},{2,3},{3,2},{4,5},{5,4},{6,7},{7,6},{8,9},{9,8},{10,11... | collective-permute-start | bytes 1572872 | tf_op jit(solution)/shard_map/ppermute | solution.py:227
  91.0 1.1 %shard_map.104.c_ref = bf16[512,1024]{1,0:T(8,128)(2,1)S(1)} custom-call(bf16[512,512]{1,0:T(8,128)(2,1)S(1)} %get-tuple-element.20.m_ref, bf16[1024,512]{1,0:T(8,128)(2,1)S(1)} %copy-done.3), custom_call_target="tpu_custom_call" | custom-call | flops 536870912 | bytes 2621440 | tf_op jit(solution)/shard_map/pallas_call | solution.py:39
  92.1 0.4 shard_map.107.sum_ref
  92.5 0.0 collective-permute-done.3.other_ref
  92.5 1.2 %shard_map.108 = bf16[512,512]{1,0:T(8,128)(2,1)} custom-call(f32[512,512]{1,0:T(8,128)S(1)} %shard_map.107.sum_ref, bf16[512,1024]{1,0:T(8,128)(2,1)S(1)} %shard_map.104.c_ref, bf16[512,512]{1,0:T(8,128)(2,1)S(1)} %collective-permute-done.3.other_ref), custom_call_target="tpu_custom_call" | custom-call | flops 268435456 | bytes 3145728 | tf_op jit(solution)/shard_map/pallas_call | solution.py:39
  (18 shorter events, 0.0 us)
Async XLA Ops:
  0.0 0.7 copy-start.13
  0.0 0.7 copy-start.12
  0.7 1.0 %copy-start.8 = (bf16[64,8,512]{2,1,0:T(8,128)(2,1)S(1)}, bf16[64,8,512]{2,1,0:T(8,128)(2,1)}, u32[]{:S(2)}) copy-start(bf16[64,8,512]{2,1,0:T(8,128)(2,1)} %param.10) | copy-start | bytes 1572868
  1.7 13.3 %copy-start.11 = (bf16[512,512]{1,0:T(8,128)(2,1)S(1)}, bf16[512,512]{1,0:T(8,128)(2,1)}, u32[]{:S(2)}) copy-start(bf16[512,512]{1,0:T(8,128)(2,1)} %wv_ref.1) | copy-start | bytes 1572868
  2.2 12.8 %copy-start.9 = (bf16[512,512]{1,0:T(8,128)(2,1)S(1)}, bf16[512,512]{1,0:T(8,128)(2,1)}, u32[]{:S(2)}) copy-start(bf16[512,512]{1,0:T(8,128)(2,1)} %wq_ref.1) | copy-start | bytes 1572868
  2.2 12.8 %copy-start.10 = (bf16[512,512]{1,0:T(8,128)(2,1)S(1)}, bf16[512,512]{1,0:T(8,128)(2,1)}, u32[]{:S(2)}) copy-start(bf16[512,512]{1,0:T(8,128)(2,1)} %wk_ref.1) | copy-start | bytes 1572868
  15.0 15.0 %copy-start.4 = (bf16[512,512]{1,0:T(8,128)(2,1)S(1)}, bf16[512,512]{1,0:T(8,128)(2,1)}, u32[]{:S(2)}) copy-start(bf16[512,512]{1,0:T(8,128)(2,1)} %wo_ref.1) | copy-start | bytes 1572868
  15.0 18.3 %copy-start.7 = (bf16[512,1024]{1,0:T(8,128)(2,1)S(1)}, bf16[512,1024]{1,0:T(8,128)(2,1)}, u32[]{:S(2)}) copy-start(bf16[512,1024]{1,0:T(8,128)(2,1)} %refs_0_.1) | copy-start | bytes 3145732
  18.8 14.5 %copy-start.1 = (bf16[1,1024,512]{2,1,0:T(8,128)(2,1)S(1)}, bf16[1,1024,512]{2,1,0:T(8,128)(2,1)}, u32[]{:S(2)}) copy-start(bf16[1,1024,512]{2,1,0:T(8,128)(2,1)} %param.19) | copy-start | bytes 3145732
  30.0 2.9 %copy-start = (bf16[1,512,1024]{2,1,0:T(8,128)(2,1)S(1)}, bf16[1,512,1024]{2,1,0:T(8,128)(2,1)}, u32[]{:S(2)}) copy-start(bf16[1,512,1024]{2,1,0:T(8,128)(2,1)} %param.18) | copy-start | bytes 3145732
  30.6 5.8 %collective-permute-start = (bf16[512,512]{1,0:T(8,128)(2,1)S(1)}, bf16[512,512]{1,0:T(8,128)(2,1)S(1)}, u32[]{:S(2)}, u32[]{:S(2)}) collective-permute-start(bf16[512,512]{1,0:T(8,128)(2,1)S(1)} %get-tuple-element.18.refs_2_.m_ref), channel_id=1, source_target_pairs={{0,1},{1,0},{2,3},{3,2},{4,5},{5,4},{6,7},{7,6},{8,9},{9,8},{10,11... | collective-permute-start | bytes 1572872 | tf_op jit(solution)/shard_map/ppermute | solution.py:227
  32.8 19.5 %collective-permute-start.1 = (bf16[512,1024]{1,0:T(8,128)(2,1)S(1)}, bf16[512,1024]{1,0:T(8,128)(2,1)}, u32[]{:S(2)}, u32[]{:S(2)}) collective-permute-start(bf16[512,1024]{1,0:T(8,128)(2,1)S(1)} %bitcast.15), channel_id=1, source_target_pairs={{0,1},{1,0},{2,3},{3,2},{4,5},{5,4},{6,7},{7,6},{8,9},{9,8},{10,11... | collective-permute-start | bytes 3145736 | tf_op jit(solution)/shard_map/ppermute | solution.py:227
  33.3 19.0 %collective-permute-start.2 = (bf16[1024,512]{1,0:T(8,128)(2,1)S(1)}, bf16[1024,512]{1,0:T(8,128)(2,1)}, u32[]{:S(2)}, u32[]{:S(2)}) collective-permute-start(bf16[1024,512]{1,0:T(8,128)(2,1)S(1)} %bitcast.17), channel_id=1, source_target_pairs={{0,1},{1,0},{2,3},{3,2},{4,5},{5,4},{6,7},{7,6},{8,9},{9,8},{10,11... | collective-permute-start | bytes 3145736 | tf_op jit(solution)/shard_map/ppermute | solution.py:227
  34.7 1.0 %copy-start.2 = (bf16[1024,512]{1,0:T(8,128)(2,1)}, bf16[1024,512]{1,0:T(8,128)(2,1)S(1)}, u32[]{:S(2)}) copy-start(bf16[1024,512]{1,0:T(8,128)(2,1)S(1)} %get-tuple-element.21.slots_ref) | copy-start | bytes 3145732
  35.7 0.8 copy-start.5
  39.0 26.8 %all-to-all-start.2 = ((bf16[16,136,128]{2,1,0:T(8,128)(2,1)}), bf16[16,136,128]{2,1,0:T(8,128)(2,1)S(1)}, u32[]{:S(2)}, u32[]{:S(2)}) async-start(bf16[16,136,128]{2,1,0:T(8,128)(2,1)} %shard_map.105), calls=%async_computation.2 | async-start | bytes 1114112 | tf_op jit(solution)/shard_map/all_to_all | solution.py:254
  68.6 22.4 %copy-start.3 = (bf16[1024,512]{1,0:T(8,128)(2,1)S(1)}, bf16[1024,512]{1,0:T(8,128)(2,1)}, u32[]{:S(2)}) copy-start(bf16[1024,512]{1,0:T(8,128)(2,1)} %copy-done.2) | copy-start | bytes 3145732
  89.9 2.6 %collective-permute-start.3 = (bf16[512,512]{1,0:T(8,128)(2,1)S(1)}, bf16[512,512]{1,0:T(8,128)(2,1)S(1)}, u32[]{:S(2)}, u32[]{:S(2)}) collective-permute-start(bf16[512,512]{1,0:T(8,128)(2,1)S(1)} %bitcast.13), channel_id=1, source_target_pairs={{0,1},{1,0},{2,3},{3,2},{4,5},{5,4},{6,7},{7,6},{8,9},{9,8},{10,11... | collective-permute-start | bytes 1572872 | tf_op jit(solution)/shard_map/ppermute | solution.py:227
  91.0 1.1 %copy-start.6 = (bf16[512,512]{1,0:T(8,128)(2,1)S(1)}, bf16[512,512]{1,0:T(8,128)(2,1)}, u32[]{:S(2)}) copy-start(bf16[512,512]{1,0:T(8,128)(2,1)} %copy-done.5) | copy-start | bytes 1572868

commit v6 on v5

--- a/solution.py
+++ b/solution.py
@@ -32,7 +32,7 @@
     return lax.dot_general(a, b, (((1,), (1,)), ((), ())), preferred_element_type=F32)
 
 
-def call(kernel, out_shape, args, scratch=(), flops=1 << 20, transcendentals=0):
+def call(kernel, out_shape, args, scratch=(), flops=1 << 20, transcendentals=0, out_left=False):
     single = isinstance(out_shape, jax.ShapeDtypeStruct)
     outs = (out_shape,) if single else tuple(out_shape)
     moved = sum(a.size * a.dtype.itemsize for a in (*args, *outs))
@@ -40,7 +40,9 @@
         kernel,
         out_shape=out_shape,
         in_specs=[VMEM] * len(args),
-        out_specs=VMEM if single else tuple([VMEM] * len(outs)),
+        out_specs=(pl.BlockSpec(memory_space=pl.ANY) if out_left else VMEM)
+        if single
+        else tuple([VMEM] * len(outs)),
         scratch_shapes=list(scratch),
         compiler_params=pltpu.CompilerParams(vmem_limit_bytes=16 << 20),
         cost_estimate=pl.CostEstimate(
@@ -153,7 +155,7 @@
     all_s[:tokens, :] = m_ref[...]
     all_s[tokens:, :] = other_ref[...]
     half = SLOTS // 2
-    rows = 256
+    rows = 512
     for start in range(0, keys_ref.shape[0], rows):
         t = nt(keys_ref[start : start + rows, :], all_s[...]) * (LOGIT_SCALE * LOG2E)
         largest = jnp.max(t, axis=1, keepdims=True)
@@ -218,9 +220,18 @@
     o_ref[...] = r_ref[...].astype(F32) + nn(c_ref[:, :count], own_ref[...])
 
 
-def output_kernel(sum_ref, c_ref, other_ref, o_ref):
+def output_kernel(sum_ref, c_ref, other_ref, o_ref, rows_s, sems):
     count = other_ref.shape[0]
-    o_ref[...] = (sum_ref[...] + nn(c_ref[:, count:], other_ref[...])).astype(BF16)
+    run = sum_ref.shape[0] // 2
+    copies = []
+    for k in range(2):
+        part = slice(k * run, (k + 1) * run)
+        rows = sum_ref[part, :] + nn(c_ref[part, count:], other_ref[...])
+        rows_s[part, :] = rows.astype(BF16)
+        copies.append(pltpu.make_async_copy(rows_s.at[part, :], o_ref.at[part, :], sems.at[k]))
+        copies[k].start()
+    for copy in copies:
+        copy.wait()
 
 
 def from_other_core(block):
@@ -323,7 +334,12 @@
         flops=2 * tokens**2 * features,
     )
     out = call(
-        output_kernel, wide, (own_sum, combine, other_half), flops=2 * tokens**2 * features
+        output_kernel,
+        wide,
+        (own_sum, combine, other_half),
+        scratch=[pltpu.VMEM((tokens, features), BF16), pltpu.SemaphoreType.DMA((2,))],
+        flops=2 * tokens**2 * features,
+        out_left=True,
     )
     return out.reshape(frame_count, pos_count, features)
 

time: 94.2 us -> 94 us (level)
  no operation moved by 1% of the time
where the time goes in v6:
time: 94 us; the launch traced here: 93.5 us
  blocking collectives  45.3 us (48%)
  starting transfers between devices  17 us (18%)
  Pallas kernels  14 us (15%)
  waiting for transfers between devices  13.6 us (14%)
  local copies, waits for them, and re-layouts  3.57 us (4%)
    all_to_all x2, blocking collectives, over_frames(): lax.all_to_all(block, 'frame', split_axis=0, concat_axis=0, tiled=True, a...  24 us
    all_to_all x1, blocking collectives, over_chips(): lax.all_to_all(blocks, 'pos', split_axis=0, concat_axis=0, tiled=True, ax...  21.3 us
    pallas_call x9, Pallas kernels, call(): pl.pallas_call(kernel, out_shape=out_shape, in_specs=[VMEM] * len(args),...  14 us
    all_to_all x1, waiting for transfers between devices, over_chips(): lax.all_to_all(blocks, 'pos', split_axis=0, concat_axis=0, tiled=True, ax...  13.5 us
    all_to_all x1, starting transfers between devices, over_chips(): lax.all_to_all(blocks, 'pos', split_axis=0, concat_axis=0, tiled=True, ax...  13.3 us
    ppermute x4, starting transfers between devices, from_other_core(): lax.ppermute(block, 'pos', [(k, k ^ 1) for k in range(lax.axis_size('pos'...  3.73 us
    unnamed x28, local copies, waits for them, and re-layouts  3.57 us
  transfers between devices with their start and end apart: 5, of which 1 were waited for; matrix products, arithmetic and copies ran while one was open for 0% of the time, Pallas kernels for 6%

profile of v6, /device:TPU:1, one launch (start us, length us, event | category | flops | bytes accessed | tf_op | source)
XLA Modules:
  0.0 93.5 jit_solution(11448554192522173206)
XLA Ops:
  0.0 0.7 copy-done.13
  0.7 0.0 copy-done.12
  0.7 1.0 %copy-done.8 = bf16[64,8,512]{2,1,0:T(8,128)(2,1)S(1)} copy-done((bf16[64,8,512]{2,1,0:T(8,128)(2,1)S(1)}, bf16[64,8,512]{2,1,0:T(8,128)(2,1)}, u32[]{:S(2)}) %copy-start.8) | copy-done | bytes 524312
  1.7 0.4 shard_map.100
  2.2 0.0 copy-start.9
  2.2 0.0 copy-start.10
  2.2 12.8 %all_to_all.20 = bf16[8,64,512]{2,1,0:T(8,128)(2,1)S(1)} all-to-all(bf16[8,64,512]{2,1,0:T(8,128)(2,1)S(1)} %bitcast.11), channel_id=1, replica_groups={{160,224,128,192,96,64,32,0},{161,225,129,193,97,65,33,1},{162,226,130,..., dimensions={0} | all-to-all | bytes 1048576 | tf_op jit(solution)/shard_map/all_to_all | solution.py:258
  15.0 0.0 copy-start.4
  15.0 0.0 copy-start.7
  15.0 3.7 %shard_map.101 = bf16[512,512]{1,0:T(8,128)(2,1)S(1)} custom-call(bf16[512,512]{1,0:T(8,128)(2,1)S(1)} %bitcast.20, f32[1,512]{1,0:T(1,128)S(1)} %get-tuple-element.15.gain_ref, bf16[512,512]{1,0:T(8,128)(2,1)S(1)} %copy-done.9, bf16[512,512]{1,0:T(8,128)(2,1)S(1)} %copy-done.10, bf16[512,512]{1,0:T(8,128)(2,1)S(1)} %copy-done.11), custom_call_target="tpu_custom_call" | custom-call | flops 1879048192 | bytes 2623488 | tf_op jit(solution)/shard_map/pallas_call | solution.py:39
  18.8 0.0 copy-start.1
  18.8 11.2 %all_to_all.21 = bf16[8,64,512]{2,1,0:T(8,128)(2,1)S(1)} all-to-all(bf16[8,64,512]{2,1,0:T(8,128)(2,1)S(1)} %bitcast.19), channel_id=1, replica_groups={{160,224,128,192,96,64,32,0},{161,225,129,193,97,65,33,1},{162,226,130,..., dimensions={0} | all-to-all | bytes 1048576 | tf_op jit(solution)/shard_map/all_to_all | solution.py:258
  30.0 0.7 shard_map.102
  30.6 2.2 %collective-permute-start = (bf16[512,512]{1,0:T(8,128)(2,1)S(1)}, bf16[512,512]{1,0:T(8,128)(2,1)S(1)}, u32[]{:S(2)}, u32[]{:S(2)}) collective-permute-start(bf16[512,512]{1,0:T(8,128)(2,1)S(1)} %get-tuple-element.18.refs_2_.m_ref), channel_id=1, source_target_pairs={{0,1},{1,0},{2,3},{3,2},{4,5},{5,4},{6,7},{7,6},{8,9},{9,8},{10,11... | collective-permute-start | bytes 1572872 | tf_op jit(solution)/shard_map/ppermute | solution.py:238
  32.8 0.5 collective-permute-start.1
  33.3 0.0 collective-permute-start.2
  33.3 1.3 %shard_map.103 = (bf16[512,512]{1,0:T(8,128)(2,1)S(1)}, bf16[1024,512]{1,0:T(8,128)(2,1)S(1)}, bf16[512,512]{1,0:T(8,128)(2,1)S(1)}, bf16[512,512]{1,0:T(8,128)(2,1)S(1)}) custom-call(bf16[512,1024]{1,0:T(8,128)(2,1)S(1)} %copy-done.7, bf16[512,512]{1,0:T(8,128)(2,1)S(1)} %get-tuple-element.17.refs_1_, bf16[512,512]{1,0:T(8,128)(2,1)S(1)} %get-tuple-element.18.refs_2_.m_ref), custom_call_target="tpu_custom_call" | custom-call | flops 671088640 | bytes 4718592 | tf_op jit(solution)/shard_map/pallas_call | solution.py:39
  34.7 1.0 %copy-done.2 = bf16[1024,512]{1,0:T(8,128)(2,1)} copy-done((bf16[1024,512]{1,0:T(8,128)(2,1)}, bf16[1024,512]{1,0:T(8,128)(2,1)S(1)}, u32[]{:S(2)}) %copy-start.2) | copy-done | bytes 1048600
  35.7 0.8 copy-done.5
  36.5 0.0 collective-permute-done.other_ref
  36.5 2.4 %shard_map.105 = bf16[16,136,128]{2,1,0:T(8,128)(2,1)} custom-call(bf16[512,512]{1,0:T(8,128)(2,1)S(1)} %get-tuple-element.18.refs_2_.m_ref, bf16[512,512]{1,0:T(8,128)(2,1)S(1)} %collective-permute-done.other_ref, bf16[512,512]{1,0:T(8,128)(2,1)S(1)} %get-tuple-element.22.keys_ref), custom_call_target="tpu_custom_call" | custom-call | flops 1073741824 | bytes 2129920 | tf_op jit(solution)/shard_map/pallas_call | solution.py:39
  38.9 13.3 %all-to-all-start.2 = ((bf16[16,136,128]{2,1,0:T(8,128)(2,1)}), bf16[16,136,128]{2,1,0:T(8,128)(2,1)S(1)}, u32[]{:S(2)}, u32[]{:S(2)}) async-start(bf16[16,136,128]{2,1,0:T(8,128)(2,1)} %shard_map.105), calls=%async_computation.2 | async-start | bytes 1114112 | tf_op jit(solution)/shard_map/all_to_all | solution.py:265
  52.2 0.0 collective-permute-done.1.other_in_ref
  52.2 0.0 collective-permute-done.2.other_out_ref
  52.2 13.5 %all-to-all-done.2.got_ref = bf16[16,136,128]{2,1,0:T(8,128)(2,1)S(1)} async-done(((bf16[16,136,128]{2,1,0:T(8,128)(2,1)}), bf16[16,136,128]{2,1,0:T(8,128)(2,1)S(1)}, u32[]{:S(2)}, u32[]{:S(2)}) %all-to-all-start.2) | async-done | bytes 557088 | tf_op jit(solution)/shard_map/all_to_all | solution.py:265
  65.7 2.7 %shard_map.106 = bf16[16,32,512]{2,1,0:T(8,128)(2,1)S(1)} custom-call(bf16[16,136,128]{2,1,0:T(8,128)(2,1)S(1)} %all-to-all-done.2.got_ref, bf16[512,1024]{1,0:T(8,128)(2,1)S(1)} %bitcast.16, bf16[512,1024]{1,0:T(8,128)(2,1)} %collective-permute-done.1.other_in_ref, bf16[1024,512]{1,0:T(8,128)(2,1)S(1)} %bitcast.18, ...), custom_call_target="tpu_custom_call" | custom-call | flops 268435456 | bytes 5275648 | tf_op jit(solution)/shard_map/pallas_call | solution.py:39
  68.5 21.3 %all_to_all.22 = bf16[16,32,512]{2,1,0:T(8,128)(2,1)S(1)} all-to-all(bf16[16,32,512]{2,1,0:T(8,128)(2,1)S(1)} %shard_map.106), channel_id=1, replica_groups={{18,22,26,30,2,6,10,14,16,20,24,28,0,4,8,12},{19,23,27,31,3,7,11,15,17,..., dimensions={0} | all-to-all | bytes 1048576 | tf_op jit(solution)/shard_map/all_to_all | solution.py:265
  89.8 1.0 %collective-permute-start.3 = (bf16[512,512]{1,0:T(8,128)(2,1)S(1)}, bf16[512,512]{1,0:T(8,128)(2,1)S(1)}, u32[]{:S(2)}, u32[]{:S(2)}) collective-permute-start(bf16[512,512]{1,0:T(8,128)(2,1)S(1)} %bitcast.13), channel_id=1, source_target_pairs={{0,1},{1,0},{2,3},{3,2},{4,5},{5,4},{6,7},{7,6},{8,9},{9,8},{10,11... | collective-permute-start | bytes 1572872 | tf_op jit(solution)/shard_map/ppermute | solution.py:238
  90.8 1.1 %shard_map.104.c_ref = bf16[512,1024]{1,0:T(8,128)(2,1)S(1)} custom-call(bf16[512,512]{1,0:T(8,128)(2,1)S(1)} %get-tuple-element.20.m_ref, bf16[1024,512]{1,0:T(8,128)(2,1)S(1)} %copy-done.3), custom_call_target="tpu_custom_call" | custom-call | flops 536870912 | bytes 2621440 | tf_op jit(solution)/shard_map/pallas_call | solution.py:39
  91.9 0.4 shard_map.107.sum_ref
  92.4 0.0 collective-permute-done.3.other_ref
  92.4 1.2 %shard_map.108 = bf16[512,512]{1,0:T(8,128)(2,1)} custom-call(f32[512,512]{1,0:T(8,128)S(1)} %shard_map.107.sum_ref, bf16[512,1024]{1,0:T(8,128)(2,1)S(1)} %shard_map.104.c_ref, bf16[512,512]{1,0:T(8,128)(2,1)S(1)} %collective-permute-done.3.other_ref), custom_call_target="tpu_custom_call" | custom-call | flops 268435456 | bytes 3145728 | tf_op jit(solution)/shard_map/pallas_call | solution.py:39
  (18 shorter events, 0.0 us)
Async XLA Ops:
  0.0 0.7 copy-start.13
  0.0 0.7 copy-start.12
  0.7 1.0 %copy-start.8 = (bf16[64,8,512]{2,1,0:T(8,128)(2,1)S(1)}, bf16[64,8,512]{2,1,0:T(8,128)(2,1)}, u32[]{:S(2)}) copy-start(bf16[64,8,512]{2,1,0:T(8,128)(2,1)} %param.10) | copy-start | bytes 1572868
  1.7 13.3 %copy-start.11 = (bf16[512,512]{1,0:T(8,128)(2,1)S(1)}, bf16[512,512]{1,0:T(8,128)(2,1)}, u32[]{:S(2)}) copy-start(bf16[512,512]{1,0:T(8,128)(2,1)} %wv_ref.1) | copy-start | bytes 1572868
  2.2 12.8 %copy-start.9 = (bf16[512,512]{1,0:T(8,128)(2,1)S(1)}, bf16[512,512]{1,0:T(8,128)(2,1)}, u32[]{:S(2)}) copy-start(bf16[512,512]{1,0:T(8,128)(2,1)} %wq_ref.1) | copy-start | bytes 1572868
  2.2 12.8 %copy-start.10 = (bf16[512,512]{1,0:T(8,128)(2,1)S(1)}, bf16[512,512]{1,0:T(8,128)(2,1)}, u32[]{:S(2)}) copy-start(bf16[512,512]{1,0:T(8,128)(2,1)} %wk_ref.1) | copy-start | bytes 1572868
  15.0 15.0 %copy-start.4 = (bf16[512,512]{1,0:T(8,128)(2,1)S(1)}, bf16[512,512]{1,0:T(8,128)(2,1)}, u32[]{:S(2)}) copy-start(bf16[512,512]{1,0:T(8,128)(2,1)} %wo_ref.1) | copy-start | bytes 1572868
  15.0 18.3 %copy-start.7 = (bf16[512,1024]{1,0:T(8,128)(2,1)S(1)}, bf16[512,1024]{1,0:T(8,128)(2,1)}, u32[]{:S(2)}) copy-start(bf16[512,1024]{1,0:T(8,128)(2,1)} %refs_0_.1) | copy-start | bytes 3145732
  18.8 14.5 %copy-start.1 = (bf16[1,1024,512]{2,1,0:T(8,128)(2,1)S(1)}, bf16[1,1024,512]{2,1,0:T(8,128)(2,1)}, u32[]{:S(2)}) copy-start(bf16[1,1024,512]{2,1,0:T(8,128)(2,1)} %param.19) | copy-start | bytes 3145732
  30.0 2.9 %copy-start = (bf16[1,512,1024]{2,1,0:T(8,128)(2,1)S(1)}, bf16[1,512,1024]{2,1,0:T(8,128)(2,1)}, u32[]{:S(2)}) copy-start(bf16[1,512,1024]{2,1,0:T(8,128)(2,1)} %param.18) | copy-start | bytes 3145732
  30.6 5.8 %collective-permute-start = (bf16[512,512]{1,0:T(8,128)(2,1)S(1)}, bf16[512,512]{1,0:T(8,128)(2,1)S(1)}, u32[]{:S(2)}, u32[]{:S(2)}) collective-permute-start(bf16[512,512]{1,0:T(8,128)(2,1)S(1)} %get-tuple-element.18.refs_2_.m_ref), channel_id=1, source_target_pairs={{0,1},{1,0},{2,3},{3,2},{4,5},{5,4},{6,7},{7,6},{8,9},{9,8},{10,11... | collective-permute-start | bytes 1572872 | tf_op jit(solution)/shard_map/ppermute | solution.py:238
  32.8 19.4 %collective-permute-start.1 = (bf16[512,1024]{1,0:T(8,128)(2,1)S(1)}, bf16[512,1024]{1,0:T(8,128)(2,1)}, u32[]{:S(2)}, u32[]{:S(2)}) collective-permute-start(bf16[512,1024]{1,0:T(8,128)(2,1)S(1)} %bitcast.15), channel_id=1, source_target_pairs={{0,1},{1,0},{2,3},{3,2},{4,5},{5,4},{6,7},{7,6},{8,9},{9,8},{10,11... | collective-permute-start | bytes 3145736 | tf_op jit(solution)/shard_map/ppermute | solution.py:238
  33.3 18.9 %collective-permute-start.2 = (bf16[1024,512]{1,0:T(8,128)(2,1)S(1)}, bf16[1024,512]{1,0:T(8,128)(2,1)}, u32[]{:S(2)}, u32[]{:S(2)}) collective-permute-start(bf16[1024,512]{1,0:T(8,128)(2,1)S(1)} %bitcast.17), channel_id=1, source_target_pairs={{0,1},{1,0},{2,3},{3,2},{4,5},{5,4},{6,7},{7,6},{8,9},{9,8},{10,11... | collective-permute-start | bytes 3145736 | tf_op jit(solution)/shard_map/ppermute | solution.py:238
  34.7 1.0 %copy-start.2 = (bf16[1024,512]{1,0:T(8,128)(2,1)}, bf16[1024,512]{1,0:T(8,128)(2,1)S(1)}, u32[]{:S(2)}) copy-start(bf16[1024,512]{1,0:T(8,128)(2,1)S(1)} %get-tuple-element.21.slots_ref) | copy-start | bytes 3145732
  35.7 0.8 copy-start.5
  38.9 26.8 %all-to-all-start.2 = ((bf16[16,136,128]{2,1,0:T(8,128)(2,1)}), bf16[16,136,128]{2,1,0:T(8,128)(2,1)S(1)}, u32[]{:S(2)}, u32[]{:S(2)}) async-start(bf16[16,136,128]{2,1,0:T(8,128)(2,1)} %shard_map.105), calls=%async_computation.2 | async-start | bytes 1114112 | tf_op jit(solution)/shard_map/all_to_all | solution.py:265
  68.5 22.4 %copy-start.3 = (bf16[1024,512]{1,0:T(8,128)(2,1)S(1)}, bf16[1024,512]{1,0:T(8,128)(2,1)}, u32[]{:S(2)}) copy-start(bf16[1024,512]{1,0:T(8,128)(2,1)} %copy-done.2) | copy-start | bytes 3145732
  89.8 2.6 %collective-permute-start.3 = (bf16[512,512]{1,0:T(8,128)(2,1)S(1)}, bf16[512,512]{1,0:T(8,128)(2,1)S(1)}, u32[]{:S(2)}, u32[]{:S(2)}) collective-permute-start(bf16[512,512]{1,0:T(8,128)(2,1)S(1)} %bitcast.13), channel_id=1, source_target_pairs={{0,1},{1,0},{2,3},{3,2},{4,5},{5,4},{6,7},{7,6},{8,9},{9,8},{10,11... | collective-permute-start | bytes 1572872 | tf_op jit(solution)/shard_map/ppermute | solution.py:238
  90.8 1.1 %copy-start.6 = (bf16[512,512]{1,0:T(8,128)(2,1)S(1)}, bf16[512,512]{1,0:T(8,128)(2,1)}, u32[]{:S(2)}) copy-start(bf16[512,512]{1,0:T(8,128)(2,1)} %copy-done.5) | copy-start | bytes 1572868
